TPU v7x, 256 devices: a whole 4x4x8 slice. The times are simulated.
256 devices in a mesh: comp: 16 (over x, y_lo, core), dom: 16 (over y_hi, z).
Axes of the slice: x: 4, y: 4 (y_hi: 2, y_lo: 2; y = y_hi * 2 + y_lo), z: 8, core: 2. Of those that a mesh axis runs over, the one named last changes fastest.
Arguments:
- density: float32 [16, 32, 16, 16, 256], P('comp', 'dom'), may hold values from -6 to 6
- velocity: bfloat16 [16, 6, 32, 16, 16, 256], P('comp', None, 'dom'), may hold values from -0.099609375 to 0.099609375
- coefficients: int32 [16], replicated, may hold values from -1 to 1, as said below
- owner_lists: int32 [388, 16], replicated, may hold values from -1 to 511, as said below
Outputs:
- combined: float32 [16, 32, 16, 16, 256], P('comp', 'dom')
Inputs may be any that keep to these rules, and one draw needn't show every extreme that they name: `coefficients`: each is -1 or 1. `owner_lists`: every slab number c * 32 + s appears in exactly one row; within a row the entries are distinct and ascending, padding -1 follows them, and every row has at least one entry; no row names two slabs of one component; 4 rows name all 16 components; exactly 68 rows have more than one entry, and those that do not name all components have exactly two; every component has exactly 12 slabs in rows with more than one entry.
All inputs are finite; a program needn't handle non-finite values.
Results may differ from a plain program's by a relative error of at most 0.0003.
Values may be sent and summed in bfloat16 or wider, within the bound.
A program may use at most 64 MiB of HBM per device.

v0:
```python
import jax
import jax.numpy as jnp
import numpy as np
from jax import lax
from jax.sharding import PartitionSpec as P

GRID_A = 32
GRID_B = 16
GRID_C = 16
GRID_D = 8
GRID_E = 8
GRID_F = 4
STEPS = 4


def with_halo(block, sides, width):
    for axis, dim in sides:
        count = lax.axis_size(axis)
        forward = [(i, i + 1) for i in range(count - 1)]
        forward.append((count - 1, 0))
        backward = [(target, source) for source, target in forward]
        low = lax.ppermute(
            lax.slice_in_dim(block, block.shape[dim] - width, None, axis=dim), axis, forward
        )
        high = lax.ppermute(lax.slice_in_dim(block, 0, width, axis=dim), axis, backward)
        block = jnp.concatenate([low, block, high], axis=dim)
    return block


def surplus_matrix(points):
    matrix = np.eye(points)
    for position in range(1, points):
        spacing = position & -position
        matrix[position, (position - spacing) % points] -= 0.5
        matrix[position, (position + spacing) % points] -= 0.5
    return matrix


def nodal_matrix(points):
    matrix = np.zeros((points, points))
    matrix[0, 0] = 1.0
    spacing = points // 2
    while spacing >= 1:
        for position in range(spacing, points, 2 * spacing):
            matrix[position] = 0.5 * (
                matrix[(position - spacing) % points] + matrix[(position + spacing) % points]
            )
            matrix[position, position] += 1.0
        spacing = spacing // 2
    return matrix


def to_lookup_table(matrix):
    return jnp.asarray(matrix, jnp.float32)


def neighbours(values, dimension):
    if dimension == 1:
        return (jnp.roll(values, -1, 2), jnp.roll(values, 1, 2))
    if dimension == 2:
        return (jnp.roll(values, -1, 3), jnp.roll(values, 1, 3))
    if dimension == 3:
        sub_stride, sub_extent = (GRID_E * GRID_F, GRID_D)
    elif dimension == 4:
        sub_stride, sub_extent = (GRID_F, GRID_E)
    else:
        sub_stride, sub_extent = (1, GRID_F)
    sub_index = lax.iota(jnp.int32, values.shape[4]) // sub_stride % sub_extent
    forward_sweep = jnp.where(
        sub_index == sub_extent - 1,
        jnp.roll(values, (sub_extent - 1) * sub_stride, 4),
        jnp.roll(values, -sub_stride, 4),
    )
    backward = jnp.where(
        sub_index == 0,
        jnp.roll(values, -(sub_extent - 1) * sub_stride, 4),
        jnp.roll(values, sub_stride, 4),
    )
    return (forward_sweep, backward)


def advance_planes(widened_grid, speeds):
    central_part = widened_grid[:, 1:-1]
    rates = speeds.astype(jnp.float32)
    forward_sweep, backward = (widened_grid[:, 2:], widened_grid[:, :-2])
    updated = (
        central_part
        + 0.06 * (forward_sweep - 2.0 * central_part + backward)
        - 0.5 * rates[:, 0] * (forward_sweep - backward)
    )
    for dimension in range(1, 6):
        forward_sweep, backward = neighbours(central_part, dimension)
        updated = (
            updated
            + 0.06 * (forward_sweep - 2.0 * central_part + backward)
            - 0.5 * rates[:, dimension] * (forward_sweep - backward)
        )
    return updated


def slab_blocks(owner_lists, comp_count, slab_count):
    block_count = owner_lists.shape[0]
    block_labels = jnp.broadcast_to(
        jnp.arange(block_count, dtype=jnp.int32)[:, None], owner_lists.shape
    )
    targets = jnp.where(owner_lists >= 0, owner_lists, comp_count * slab_count)
    empty = jnp.zeros((comp_count * slab_count,), jnp.int32)
    return empty.at[targets.reshape(-1)].set(block_labels.reshape(-1), mode="drop")


def local(density, velocity, coefficients, owner_lists):
    highest = lax.Precision.HIGHEST
    comp_index = lax.axis_index("comp")
    comp_count = lax.axis_size("comp")
    current = density
    for time_step in range(STEPS):
        widened_grid = with_halo(current, (("dom", 1),), 1)
        current = advance_planes(widened_grid, velocity)
    inner_surplus = to_lookup_table(
        np.kron(np.kron(surplus_matrix(GRID_D), surplus_matrix(GRID_E)), surplus_matrix(GRID_F))
    )
    surplus = jnp.einsum("cpabl,ml->cpabm", current, inner_surplus, precision=highest)
    surplus = jnp.einsum(
        "cpabl,xa->cpxbl", surplus, to_lookup_table(surplus_matrix(GRID_B)), precision=highest
    )
    surplus = jnp.einsum(
        "cpabl,yb->cpayl", surplus, to_lookup_table(surplus_matrix(GRID_C)), precision=highest
    )
    first_surplus = to_lookup_table(surplus_matrix(GRID_A))
    columns = jnp.einsum(
        "cpabl,qp->cqabl",
        lax.all_to_all(surplus, "dom", split_axis=2, concat_axis=1, tiled=True),
        first_surplus,
        precision=highest,
    )
    column_width = columns.shape[2] * columns.shape[3] * columns.shape[4]
    slab_rows = columns.reshape(GRID_A, column_width)
    all_blocks = slab_blocks(owner_lists, comp_count, GRID_A)
    own_blocks = lax.dynamic_slice_in_dim(all_blocks, comp_index * GRID_A, GRID_A)
    weights = coefficients.astype(jnp.float32)
    own_weight = lax.dynamic_slice_in_dim(weights, comp_index, 1)
    block_terms = (
        jnp.zeros((owner_lists.shape[0], column_width), jnp.float32)
        .at[own_blocks]
        .set(slab_rows * own_weight[0])
    )
    summed = lax.psum(block_terms, "comp")
    merged = summed[own_blocks]
    nodal = jnp.einsum(
        "cpabl,qp->cqabl",
        merged.reshape(columns.shape),
        to_lookup_table(nodal_matrix(GRID_A)),
        precision=highest,
    )
    inner_nodal = to_lookup_table(
        np.kron(np.kron(nodal_matrix(GRID_D), nodal_matrix(GRID_E)), nodal_matrix(GRID_F))
    )
    second_nodal = to_lookup_table(nodal_matrix(GRID_B))
    values = lax.all_to_all(nodal, "dom", split_axis=1, concat_axis=2, tiled=True)
    values = jnp.einsum("cpabl,ml->cpabm", values, inner_nodal, precision=highest)
    planes = jnp.einsum("cpabl,xa->cpxbl", values, second_nodal, precision=highest)
    return jnp.einsum(
        "cpabl,yb->cpayl", planes, to_lookup_table(nodal_matrix(GRID_C)), precision=highest
    )


def solution(mesh):
    in_specs = (
        P("comp", "dom", None, None, None),
        P("comp", None, "dom", None, None, None),
        P(),
        P(),
    )
    out_specs = P("comp", "dom", None, None, None)
    return jax.shard_map(local, mesh=mesh, in_specs=in_specs, out_specs=out_specs, check_vma=False)
```

profile of v0, /device:TPU:1, one launch (start us, length us, event | category | flops | bytes accessed | tf_op | source)
XLA Modules:
  0.0 320.9 jit_solution(14734509411854693830)
XLA Ops:
  6.5 1.1 fusion.68
  7.7 9.1 %collective-permute-start = (f32[1,1,16,16,256]{4,3,2,1,0:T(8,128)S(1)}, f32[1,1,16,16,256]{4,3,2,1,0:T(8,128)S(1)}, u32[]{:S(2)}, u32[]{:S(2)}) collective-permute-start(f32[1,1,16,16,256]{4,3,2,1,0:T(8,128)S(1)} %get-tuple-element.95), channel_id=1, source_target_pairs={{1,0},{2,1},{3,2},{4,3},{5,4},{6,5},{7,6},{8,7},{9,8},{10,9},{11,1... | collective-permute-start | bytes 786440 | tf_op jit(solution)/shard_map/ppermute | solution.py:25
  16.8 1.3 fusion.71
  18.1 1.4 fusion.73
  19.5 1.4 fusion.76
  21.1 0.2 fusion.80
  21.4 0.2 fusion.81
  22.4 0.4 convert_element_type.4
  22.9 4.4 %collective-permute-done.1 = f32[1,1,16,16,256]{4,3,2,1,0:T(8,128)S(1)} collective-permute-done((f32[1,1,16,16,256]{4,3,2,1,0:T(8,128)S(1)}, f32[1,1,16,16,256]{4,3,2,1,0:T(8,128)S(1)}, u32[]{:S(2)}, u32[]{:S(2)}) %collective-permute-start.1) | collective-permute-done | bytes 262176 | tf_op jit(solution)/shard_map/ppermute | solution.py:22
  27.3 2.2 multiply_subtract_fusion.2
  29.8 0.2 fusion.61
  30.2 0.2 fusion.65
  31.4 0.9 collective-permute-start.2
  32.3 0.7 collective-permute-start.3
  33.1 4.5 %collective-permute-done.2 = f32[1,1,16,16,256]{4,3,2,1,0:T(8,128)S(1)} collective-permute-done((f32[1,1,16,16,256]{4,3,2,1,0:T(8,128)S(1)}, f32[1,1,16,16,256]{4,3,2,1,0:T(8,128)S(1)}, u32[]{:S(2)}, u32[]{:S(2)}) %collective-permute-start.2) | collective-permute-done | bytes 262176 | tf_op jit(solution)/shard_map/ppermute | solution.py:25
  37.6 4.7 %collective-permute-done.3 = f32[1,1,16,16,256]{4,3,2,1,0:T(8,128)S(1)} collective-permute-done((f32[1,1,16,16,256]{4,3,2,1,0:T(8,128)S(1)}, f32[1,1,16,16,256]{4,3,2,1,0:T(8,128)S(1)}, u32[]{:S(2)}, u32[]{:S(2)}) %collective-permute-start.3) | collective-permute-done | bytes 262176 | tf_op jit(solution)/shard_map/ppermute | solution.py:22
  42.3 2.2 multiply_subtract_fusion.1
  44.7 0.2 fusion.46
  45.0 0.2 fusion.47
  45.2 0.2 fusion.50
  46.4 0.4 collective-permute-start.4
  46.7 1.2 collective-permute-start.5
  48.1 3.6 %collective-permute-done.4 = f32[1,1,16,16,256]{4,3,2,1,0:T(8,128)S(1)} collective-permute-done((f32[1,1,16,16,256]{4,3,2,1,0:T(8,128)S(1)}, f32[1,1,16,16,256]{4,3,2,1,0:T(8,128)S(1)}, u32[]{:S(2)}, u32[]{:S(2)}) %collective-permute-start.4) | collective-permute-done | bytes 262176 | tf_op jit(solution)/shard_map/ppermute | solution.py:25
  51.7 3.9 %collective-permute-done.5 = f32[1,1,16,16,256]{4,3,2,1,0:T(8,128)S(1)} collective-permute-done((f32[1,1,16,16,256]{4,3,2,1,0:T(8,128)S(1)}, f32[1,1,16,16,256]{4,3,2,1,0:T(8,128)S(1)}, u32[]{:S(2)}, u32[]{:S(2)}) %collective-permute-start.5) | collective-permute-done | bytes 262176 | tf_op jit(solution)/shard_map/ppermute | solution.py:22
  55.6 2.2 multiply_subtract_fusion
  59.7 0.6 collective-permute-start.6
  60.3 0.9 collective-permute-start.7
  61.4 3.6 %collective-permute-done.6 = f32[1,1,16,16,256]{4,3,2,1,0:T(8,128)S(1)} collective-permute-done((f32[1,1,16,16,256]{4,3,2,1,0:T(8,128)S(1)}, f32[1,1,16,16,256]{4,3,2,1,0:T(8,128)S(1)}, u32[]{:S(2)}, u32[]{:S(2)}) %collective-permute-start.6) | collective-permute-done | bytes 262176 | tf_op jit(solution)/shard_map/ppermute | solution.py:25
  65.0 4.2 %collective-permute-done.7 = f32[1,1,16,16,256]{4,3,2,1,0:T(8,128)S(1)} collective-permute-done((f32[1,1,16,16,256]{4,3,2,1,0:T(8,128)S(1)}, f32[1,1,16,16,256]{4,3,2,1,0:T(8,128)S(1)}, u32[]{:S(2)}, u32[]{:S(2)}) %collective-permute-start.7) | collective-permute-done | bytes 262176 | tf_op jit(solution)/shard_map/ppermute | solution.py:22
  69.2 2.3 subtract_bitcast_fusion
  71.5 0.8 fusion.16
  72.3 0.6 convolution_bitcast_fusion.4
  72.9 0.8 convolution_bitcast_fusion.3
  73.7 0.8 copy.31
  74.6 3.6 %all-to-all-start = ((f32[1,2,16,16,256]{4,3,1,0,2:T(8,128)}), f32[1,2,16,16,256]{4,3,1,0,2:T(8,128)S(1)}, u32[]{:S(2)}, u32[]{:S(2)}) async-start(f32[1,2,16,16,256]{4,3,1,0,2:T(8,128)} %copy.31), calls=%async_computation | async-start | bytes 1048576 | tf_op jit(solution)/shard_map/all_to_all | solution.py:132
  78.7 0.6 dynamic_slice.7
  79.3 29.9 %scatter_custom_fusion = s32[512]{0:T(512)S(1)} fusion(s32[6208]{0:T(1024)S(1)} %fusion.18, s32[6208]{0:T(1024)S(1)} %reshape.2315, s32[]{:T(128)} %constant.130.clone.1), kind=kCustom, calls=%fused_computation.99 | custom fusion | bytes 2052 | tf_op jit(solution)/shard_map/scatter | solution.py:108
  109.3 0.3 copy.41
  109.7 1.1 fusion
  110.8 4.0 %scatter_custom_fusion.1 = f32[388,4096]{1,0:T(8,128)} fusion(s32[32]{0:T(128)S(1)} %compare_select_fusion.2, f32[32,4096]{1,0:T(8,128)S(1)} %fusion, f32[]{:T(128)} %constant.129.clone.1), kind=kCustom, calls=%fused_computation.5 | custom fusion | bytes 6356996 | tf_op jit(solution)/shard_map/scatter | solution.py:145
  114.9 167.1 %all-reduce.2.cloned.1.call-done = f32[388,4096]{1,0:T(8,128)} async-done(((f32[388,4096]{1,0:T(8,128)}), f32[388,4096]{1,0:T(8,128)}) %all-reduce.2.cloned.1.call-update) | async-done | bytes 6357008 | tf_op jit(solution)/shard_map/psum | solution.py:147
  282.0 3.8 %gather_fusion = f32[32,4096]{1,0:T(8,128)S(1)} fusion(f32[388,4096]{1,0:T(8,128)} %all-reduce.2.cloned.1.call-done, s32[1024]{0:T(1024)S(1)} %pad_clamp_fusion), kind=kCustom, calls=%fused_computation | custom fusion | bytes 1048704 | tf_op jit(solution)/shard_map/gather | solution.py:148
  285.8 0.6 convolution_bitcast_fusion.2
  286.3 0.3 copy.33
  286.7 24.4 %all_to_all.30 = f32[1,32,1,16,256]{4,3,2,0,1:T(8,128)S(1)} all-to-all(f32[1,32,1,16,256]{4,3,2,0,1:T(8,128)S(1)} %copy.33), channel_id=1, replica_groups=mesh['comp'=16,'dom'=16] {'dom'}, dimensions={1} | all-to-all | bytes 1048576 | tf_op jit(solution)/shard_map/all_to_all | solution.py:159
  311.0 0.8 fusion.11
  311.9 0.6 convolution_bitcast_fusion.1
  312.5 1.6 convolution_bitcast_fusion
  (85 shorter events, 6.7 us)
Async XLA Ops:
  6.5 14.4 %copy-start = (f32[1,2,16,16,256]{4,3,2,1,0:T(8,128)S(1)}, f32[1,2,16,16,256]{4,3,2,1,0:T(8,128)}, u32[]{:S(2)}) copy-start(f32[1,2,16,16,256]{4,3,2,1,0:T(8,128)} %param.12) | copy-start | bytes 1572868
  7.7 15.2 %collective-permute-start = (f32[1,1,16,16,256]{4,3,2,1,0:T(8,128)S(1)}, f32[1,1,16,16,256]{4,3,2,1,0:T(8,128)S(1)}, u32[]{:S(2)}, u32[]{:S(2)}) collective-permute-start(f32[1,1,16,16,256]{4,3,2,1,0:T(8,128)S(1)} %get-tuple-element.95), channel_id=1, source_target_pairs={{1,0},{2,1},{3,2},{4,3},{5,4},{6,5},{7,6},{8,7},{9,8},{10,9},{11,1... | collective-permute-start | bytes 786440 | tf_op jit(solution)/shard_map/ppermute | solution.py:25
  16.8 10.5 %collective-permute-start.1 = (f32[1,1,16,16,256]{4,3,2,1,0:T(8,128)S(1)}, f32[1,1,16,16,256]{4,3,2,1,0:T(8,128)S(1)}, u32[]{:S(2)}, u32[]{:S(2)}) collective-permute-start(f32[1,1,16,16,256]{4,3,2,1,0:T(8,128)S(1)} %get-tuple-element.96), channel_id=1, source_target_pairs={{0,1},{1,2},{2,3},{3,4},{4,5},{5,6},{6,7},{7,8},{8,9},{9,10},{10,1... | collective-permute-start | bytes 786440 | tf_op jit(solution)/shard_map/ppermute | solution.py:22
  20.9 1.4 copy-start.1
  31.4 6.1 %collective-permute-start.2 = (f32[1,1,16,16,256]{4,3,2,1,0:T(8,128)S(1)}, f32[1,1,16,16,256]{4,3,2,1,0:T(8,128)S(1)}, u32[]{:S(2)}, u32[]{:S(2)}) collective-permute-start(f32[1,1,16,16,256]{4,3,2,1,0:T(8,128)S(1)} %get-tuple-element.65), channel_id=1, source_target_pairs={{1,0},{2,1},{3,2},{4,3},{5,4},{6,5},{7,6},{8,7},{9,8},{10,9},{11,1... | collective-permute-start | bytes 786440 | tf_op jit(solution)/shard_map/ppermute | solution.py:25
  32.3 10.0 %collective-permute-start.3 = (f32[1,1,16,16,256]{4,3,2,1,0:T(8,128)S(1)}, f32[1,1,16,16,256]{4,3,2,1,0:T(8,128)S(1)}, u32[]{:S(2)}, u32[]{:S(2)}) collective-permute-start(f32[1,1,16,16,256]{4,3,2,1,0:T(8,128)S(1)} %get-tuple-element.66), channel_id=1, source_target_pairs={{0,1},{1,2},{2,3},{3,4},{4,5},{5,6},{6,7},{7,8},{8,9},{9,10},{10,1... | collective-permute-start | bytes 786440 | tf_op jit(solution)/shard_map/ppermute | solution.py:22
  46.4 5.3 %collective-permute-start.4 = (f32[1,1,16,16,256]{4,3,2,1,0:T(8,128)S(1)}, f32[1,1,16,16,256]{4,3,2,1,0:T(8,128)S(1)}, u32[]{:S(2)}, u32[]{:S(2)}) collective-permute-start(f32[1,1,16,16,256]{4,3,2,1,0:T(8,128)S(1)} %get-tuple-element.35), channel_id=1, source_target_pairs={{1,0},{2,1},{3,2},{4,3},{5,4},{6,5},{7,6},{8,7},{9,8},{10,9},{11,1... | collective-permute-start | bytes 786440 | tf_op jit(solution)/shard_map/ppermute | solution.py:25
  46.7 8.8 %collective-permute-start.5 = (f32[1,1,16,16,256]{4,3,2,1,0:T(8,128)S(1)}, f32[1,1,16,16,256]{4,3,2,1,0:T(8,128)S(1)}, u32[]{:S(2)}, u32[]{:S(2)}) collective-permute-start(f32[1,1,16,16,256]{4,3,2,1,0:T(8,128)S(1)} %get-tuple-element.36), channel_id=1, source_target_pairs={{0,1},{1,2},{2,3},{3,4},{4,5},{5,6},{6,7},{7,8},{8,9},{9,10},{10,1... | collective-permute-start | bytes 786440 | tf_op jit(solution)/shard_map/ppermute | solution.py:22
  59.7 5.3 %collective-permute-start.6 = (f32[1,1,16,16,256]{4,3,2,1,0:T(8,128)S(1)}, f32[1,1,16,16,256]{4,3,2,1,0:T(8,128)S(1)}, u32[]{:S(2)}, u32[]{:S(2)}) collective-permute-start(f32[1,1,16,16,256]{4,3,2,1,0:T(8,128)S(1)} %get-tuple-element.5), channel_id=1, source_target_pairs={{1,0},{2,1},{3,2},{4,3},{5,4},{6,5},{7,6},{8,7},{9,8},{10,9},{11,1... | collective-permute-start | bytes 786440 | tf_op jit(solution)/shard_map/ppermute | solution.py:25
  60.3 8.8 %collective-permute-start.7 = (f32[1,1,16,16,256]{4,3,2,1,0:T(8,128)S(1)}, f32[1,1,16,16,256]{4,3,2,1,0:T(8,128)S(1)}, u32[]{:S(2)}, u32[]{:S(2)}) collective-permute-start(f32[1,1,16,16,256]{4,3,2,1,0:T(8,128)S(1)} %get-tuple-element.6), channel_id=1, source_target_pairs={{0,1},{1,2},{2,3},{3,4},{4,5},{5,6},{6,7},{7,8},{8,9},{9,10},{10,1... | collective-permute-start | bytes 786440 | tf_op jit(solution)/shard_map/ppermute | solution.py:22
  69.2 2.3 copy-start.3
  69.2 3.1 copy-start.5
  69.2 9.0 %copy-start.9 = (s32[16]{0:T(128)S(1)}, s32[16]{0:T(128)}, u32[]{:S(2)}) copy-start(s32[16]{0:T(128)} %param.14) | copy-start | bytes 196
  69.2 9.0 %copy-start.6 = (s32[388,16]{0,1:T(8,128)S(1)}, s32[388,16]{0,1:T(8,128)}, u32[]{:S(2)}) copy-start(s32[388,16]{0,1:T(8,128)} %param.15) | copy-start | bytes 74500
  71.5 38.2 %copy-start.8 = (f32[32,32]{1,0:T(8,128)S(1)}, f32[32,32]{1,0:T(8,128)}, u32[]{:S(2)}) copy-start(f32[32,32]{1,0:T(8,128)} %constant.149.clone) | copy-start | bytes 12292
  74.6 34.8 %all-to-all-start = ((f32[1,2,16,16,256]{4,3,1,0,2:T(8,128)}), f32[1,2,16,16,256]{4,3,1,0,2:T(8,128)S(1)}, u32[]{:S(2)}, u32[]{:S(2)}) async-start(f32[1,2,16,16,256]{4,3,1,0,2:T(8,128)} %copy.31), calls=%async_computation | async-start | bytes 1048576 | tf_op jit(solution)/shard_map/all_to_all | solution.py:132
  78.2 203.8 %all-reduce.2.cloned.1.call-start = ((), (), s32[]{:S(2)}) async-start(), calls=%async_computation.2 | async-start | bytes 12845056 | tf_op jit(solution)/shard_map/psum | solution.py:147
  114.8 170.9 %copy-start.7 = (f32[32,32,1]{1,0,2:T(8,128)S(1)}, f32[32,32,1]{1,0,2:T(8,128)}, u32[]{:S(2)}) copy-start(f32[32,32,1]{1,0,2:T(8,128)} %constant.156) | copy-start | bytes 12292
  114.8 196.2 %copy-start.2 = (f32[256,256,1,1]{1,0,3,2:T(8,128)S(1)}, f32[256,256,1,1]{1,0,3,2:T(8,128)}, u32[]{:S(2)}) copy-start(f32[256,256,1,1]{1,0,3,2:T(8,128)} %constant.159) | copy-start | bytes 786436
  114.8 197.1 %copy-start.4 = (f32[16,16,1,1]{1,0,3,2:T(8,128)S(1)}, f32[16,16,1,1]{1,0,3,2:T(8,128)}, u32[]{:S(2)}) copy-start(f32[16,16,1,1]{1,0,3,2:T(8,128)} %constant.155) | copy-start | bytes 3076
Sparse Core Ops, SparseCore 0:
  115.0 166.9 all-reduce.1
where the time goes:
time: 321 us
  waiting for transfers between devices  196 us (61%)
  local copies, waits for them, and re-layouts  53 us (17%)
  blocking collectives  24.4 us (8%)
  starting transfers between devices  17.4 us (5%)
  between operations  13.9 us (4%)
  other arithmetic  9.37 us (3%)
  matrix products  6.94 us (2%)
    psum x1, waiting for transfers between devices, local(): summed = lax.psum(block_terms, 'comp')  167 us
    scatter x1, local copies, waits for them, and re-layouts, slab_blocks(): empty.at[targets.reshape(-1)].set(block_labels.reshape(-1), mode='drop')  29.9 us
    all_to_all x1, blocking collectives, local(): lax.all_to_all(nodal, 'dom', split_axis=1, concat_axis=2, tiled=True)  24.4 us
    ppermute x4, waiting for transfers between devices, with_halo(): lax.ppermute(lax.slice_in_dim(block, block.shape[dim] - width, None, axis...  17.1 us
    ppermute x4, waiting for transfers between devices, with_halo(): lax.ppermute(lax.slice_in_dim(block, 0, width, axis=dim), axis, backward)  11.7 us
    ppermute x4, starting transfers between devices, with_halo(): lax.ppermute(lax.slice_in_dim(block, 0, width, axis=dim), axis, backward)  11 us
    slice x24, local copies, waits for them, and re-layouts, neighbours(): jnp.roll(values, (sub_extent - 1) * sub_stride, 4)  6.55 us
    sub x3, other arithmetic, advance_planes(): updated + 0.06 * (forward_sweep - 2.0 * central_part + backward)  6.51 us
  transfers between devices with their start and end apart: 10, of which 8 were waited for; matrix products, arithmetic and copies ran while one was open for 12% of the time, Pallas kernels for 0%

commit v1 on v0

v1 whole, which is shorter than its diff:
```python
import functools

import jax
import jax.numpy as jnp
import numpy as np
from jax import lax
from jax.experimental import pallas as pl
from jax.experimental.pallas import tpu as pltpu
from jax.sharding import PartitionSpec as P

STEPS = 4
E_STRIDE, E_EXT = 4, 8
F_STRIDE, F_EXT = 1, 4
ROWS = 16
USED = 12
CHUNKS = 4


def tables(owner_lists, coefficients, n_comp, n_slab, me):
    blocks = owner_lists.shape[0]
    shared = owner_lists[:, 1:2] >= 0
    keys = jnp.where(shared, owner_lists, -1)
    ids = jnp.arange(1, blocks + 1, dtype=jnp.int32)
    slabs = jnp.arange(n_comp * n_slab, dtype=jnp.int32)
    hit = jnp.where(keys[None] == slabs[:, None, None], ids[None, :, None], 0)
    block = jnp.sum(hit, axis=(1, 2)).reshape(n_comp, n_slab)
    multi = block > 0
    place = jnp.arange(n_slab, dtype=jnp.int32)
    before = place[None, :] < place[:, None]
    rank = jnp.sum(jnp.where(before[None] & multi[:, None, :], 1, 0), axis=2)
    slot = jnp.arange(ROWS, dtype=jnp.int32)
    chosen = multi[:, None, :] & (rank[:, None, :] == slot[None, :, None])
    row_block = jnp.sum(jnp.where(chosen, block[:, None, :], 0), axis=2)
    row_place = jnp.sum(jnp.where(chosen, place[None, None, :], 0), axis=2)
    my_rows = lax.dynamic_slice_in_dim(row_place, me, 1)[0]
    my_slot = jnp.where(
        lax.dynamic_slice_in_dim(multi, me, 1)[0],
        lax.dynamic_slice_in_dim(rank, me, 1)[0],
        USED,
    )
    weight = jnp.broadcast_to(coefficients[:, None], (n_comp, ROWS))
    flat = row_block.reshape(1, -1)
    return (
        my_rows,
        my_slot,
        flat.reshape(-1, 1),
        flat,
        weight.reshape(1, -1),
        lax.dynamic_slice_in_dim(coefficients, me, 1),
    )


def stencil(cur, low, high, left, right, rates, masks):
    e_last, e_first, f_last, f_first, d_low, d_high = masks
    out = []
    down = [pltpu.roll(x, 32, 1) for x in cur]
    up = [pltpu.roll(x, 96, 1) for x in cur]
    for h in range(2):
        x = cur[h]
        pairs = [(high[h], low[h]), (right[h], left[h])]
        n = x.shape[0]
        pairs.append((pltpu.roll(x, n - 1, 0), pltpu.roll(x, 1, 0)))
        pairs.append(
            (jnp.where(d_high, up[1 - h], up[h]), jnp.where(d_low, down[1 - h], down[h]))
        )
        pairs.append(
            (
                jnp.where(e_last, pltpu.roll(x, 28, 1), pltpu.roll(x, 124, 1)),
                jnp.where(e_first, pltpu.roll(x, 100, 1), pltpu.roll(x, 4, 1)),
            )
        )
        pairs.append(
            (
                jnp.where(f_last, pltpu.roll(x, 3, 1), pltpu.roll(x, 127, 1)),
                jnp.where(f_first, pltpu.roll(x, 125, 1), pltpu.roll(x, 1, 1)),
            )
        )
        total = None
        drift = None
        for d, (fwd, bwd) in enumerate(pairs):
            s = fwd + bwd
            m = rates[h][d] * (fwd - bwd)
            total = s if total is None else total + s
            drift = m if drift is None else drift + m
        out.append(0.28 * x + 0.06 * total - 0.5 * drift)
    return out


def kernel(
    nc, nd,
    rows_ref, slot_ref, own_ref, bcol_ref, brow_ref, wrow_ref, dens_ref, vel_ref,
    out_ref,
    ubuf, hfirst, hs, hr, line, tsend, tall, eback, erecv, ez, osend, orecv, mix,
    hs_sem, hr_sem, a_sem, b_sem,
):
    mc = lax.axis_index("comp")
    md = lax.axis_index("dom")
    nb = dens_ref.shape[1]
    size = nb // CHUNKS
    up_d = lax.rem(md + 1, nd)
    dn_d = lax.rem(md + nd - 1, nd)

    barrier = pltpu.get_barrier_semaphore()

    @pl.loop(1, nd)
    def _(i):
        pl.semaphore_signal(barrier, inc=1, device_id={"dom": lax.rem(md + i, nd)})

    @pl.loop(1, nc)
    def _(i):
        pl.semaphore_signal(barrier, inc=1, device_id={"comp": lax.rem(mc + i, nc)})

    def halo(step, way, ch):
        part = pl.ds(ch * size, size)
        if step == 0:
            src, dst = dens_ref.at[1 - way, part], hfirst.at[way, part]
        else:
            src, dst = hs.at[step - 1, way, part], hr.at[step - 1, way, part]
        return pltpu.make_async_remote_copy(
            src_ref=src,
            dst_ref=dst,
            send_sem=hs_sem.at[step, way, ch],
            recv_sem=hr_sem.at[step, way, ch],
            device_id={"dom": up_d if way == 0 else dn_d},
        )

    pl.semaphore_wait(barrier, nd + nc - 2)

    @pl.loop(0, CHUNKS)
    def _(ch):
        halo(0, 0, ch).start()
        halo(0, 1, ch).start()

    same = (bcol_ref[...] == brow_ref[...]) & (brow_ref[...] > 0)
    width = nc * ROWS
    far = (lax.broadcasted_iota(jnp.int32, (width, width), 0) // ROWS) != (
        lax.broadcasted_iota(jnp.int32, (width, width), 1) // ROWS
    )
    mix[...] = jnp.where(
        same & far, wrow_ref[...].astype(jnp.float32), 0.0
    ).astype(jnp.bfloat16)

    nrow = dens_ref.shape[2]
    lane = lax.broadcasted_iota(jnp.int32, (nrow, 128), 1)
    e_idx = (lane // E_STRIDE) % E_EXT
    f_idx = lane % F_EXT
    masks = (
        e_idx == E_EXT - 1, e_idx == 0, f_idx == F_EXT - 1, f_idx == 0,
        lane < 32, lane >= 96,
    )

    def halves(ref, *idx):
        return [ref[(*idx, slice(None), pl.ds(h * 128, 128))].astype(jnp.float32) for h in range(2)]

    for step in range(STEPS):
        src = dens_ref if step == 0 else ubuf.at[(step - 1) % 2]
        dst = ubuf.at[step % 2]

        @pl.loop(0, CHUNKS)
        def _(ch):
            halo(step, 0, ch).wait_recv()
            halo(step, 1, ch).wait_recv()

            @pl.loop(0, size)
            def _(i):
                b = ch * size + i
                bm = lax.rem(b + nb - 1, nb)
                bp = lax.rem(b + 1, nb)
                first = halves(src, 0, b)
                second = halves(src, 1, b)
                lo = halves(hfirst, 0, b) if step == 0 else halves(hr, step - 1, 0, b)
                hi = halves(hfirst, 1, b) if step == 0 else halves(hr, step - 1, 1, b)
                for p in range(2):
                    cur = first if p == 0 else second
                    rates = [
                        [
                            vel_ref[d, p, b, :, pl.ds(h * 128, 128)].astype(jnp.float32)
                            for d in range(6)
                        ]
                        for h in range(2)
                    ]
                    new = stencil(
                        cur,
                        lo if p == 0 else first,
                        second if p == 0 else hi,
                        halves(src, p, bm),
                        halves(src, p, bp),
                        rates,
                        masks,
                    )
                    for h in range(2):
                        dst[p, b, :, pl.ds(h * 128, 128)] = new[h]
                        if step < STEPS - 1:
                            hs[step, 1 - p, b, :, pl.ds(h * 128, 128)] = new[h].astype(
                                jnp.bfloat16
                            )

            if step < STEPS - 1:
                halo(step + 1, 0, ch).start()
                halo(step + 1, 1, ch).start()

    last = ubuf.at[(STEPS - 1) % 2]

    def spread(src_of, dst, phase, axis, me, peer):
        return pltpu.make_async_remote_copy(
            src_ref=src_of(peer),
            dst_ref=dst(me),
            send_sem=a_sem.at[phase, peer],
            recv_sem=b_sem.at[phase, me],
            device_id={axis: peer},
        )

    def incoming(src_of, dst, phase, axis, peer):
        return pltpu.make_async_remote_copy(
            src_ref=src_of(peer),
            dst_ref=dst(peer),
            send_sem=a_sem.at[phase, peer],
            recv_sem=b_sem.at[phase, peer],
            device_id={axis: peer},
        )

    def exchange_start(src_of, dst, phase, axis, me, n):
        @pl.loop(1, n)
        def _(i):
            spread(src_of, dst, phase, axis, me, lax.rem(me + i, n)).start()

    def exchange_wait(src_of, dst, phase, axis, me, n):
        @pl.loop(1, n)
        def _(i):
            incoming(src_of, dst, phase, axis, lax.rem(me + n - i, n)).wait_recv()

    ph0 = (lambda d: last.at[:, d], lambda d: line.at[pl.ds(2 * d, 2)], 0, "dom")
    exchange_start(*ph0, md, nd)
    for p in range(2):
        line[2 * md + p] = last[p, md]
    exchange_wait(*ph0, md, nd)

    for half in range(2):
        rows = []
        for k in range(8):
            j = half * 8 + k
            if j >= USED:
                rows.append(jnp.zeros_like(line[0]))
                continue
            s = rows_ref[j]
            h = s & (-s)
            w = jnp.where(s == 0, 0.0, 0.5)
            n = 2 * nd
            lo = (s - h) & (n - 1)
            hi = (s + h) & (n - 1)
            rows.append(line[s] - w * (line[lo] + line[hi]))
        block = jnp.stack(rows, axis=0)
        tsend[:, pl.ds(half * 8, 8), :] = jnp.swapaxes(block, 0, 1)

    ph1 = (lambda c: tsend.at[c], lambda c: tall.at[c], 1, "comp")
    exchange_start(*ph1, mc, nc)
    tall[mc] = tsend[mc]
    exchange_wait(*ph1, mc, nc)

    t = tall[...].reshape(nc * ROWS, 256)
    m = mix[...]
    acc = None
    for part in range(3):
        piece = t.astype(jnp.bfloat16)
        t = t - piece.astype(jnp.float32)
        prod = jnp.dot(m, piece, preferred_element_type=jnp.float32)
        acc = prod if acc is None else acc + prod
    eback[...] = acc.reshape(nc, ROWS, 256)

    ph2 = (lambda c: eback.at[c], lambda c: erecv.at[c], 2, "comp")
    exchange_start(*ph2, mc, nc)
    erecv[mc] = eback[mc]
    exchange_wait(*ph2, mc, nc)

    for half in range(2):
        ez[pl.ds(half * 8, 8)] = jnp.swapaxes(erecv[:, pl.ds(half * 8, 8), :], 0, 1)

    n = 2 * nd
    for q in range(4):
        if q % 2 * 8 >= nrow:
            continue
        r = (pl.ds(q % 2 * 8, min(8, nrow)), pl.ds(q // 2 * 128, 128))
        planes = {}
        planes[0] = ez[(slot_ref[0], *r)]
        gap = n // 2
        while gap >= 1:
            for s in range(gap, n, 2 * gap):
                planes[s] = ez[(slot_ref[s], *r)] + 0.5 * (
                    planes[(s - gap) % n] + planes[(s + gap) % n]
                )
            gap //= 2
        for s in range(n):
            osend[(s, *r)] = planes[s]

    ph3 = (lambda d: osend.at[pl.ds(2 * d, 2)], lambda d: orecv.at[d], 3, "dom")
    exchange_start(*ph3, md, nd)
    for p in range(2):
        orecv[md, p] = osend[2 * md + p]
    exchange_wait(*ph3, md, nd)

    own = own_ref[0].astype(jnp.float32)

    @pl.loop(0, nb)
    def _(b):
        for p in range(2):
            out_ref[p, b] = own * last[p, b] + orecv[b, p]

    @pl.loop(0, CHUNKS)
    def _(ch):
        for step in range(STEPS):
            halo(step, 0, ch).wait_send()
            halo(step, 1, ch).wait_send()

    for ph, me, k in ((ph0, md, nd), (ph1, mc, nc), (ph2, mc, nc), (ph3, md, nd)):
        @pl.loop(1, k)
        def _(i):
            spread(*ph, me, lax.rem(me + i, k)).wait_send()


def local(density, velocity, coefficients, owner_lists):
    nc = lax.axis_size("comp")
    nd = lax.axis_size("dom")
    _, planes, nb, nrow, lanes = density.shape
    tabs = tables(owner_lists, coefficients, nc, planes * nd, lax.axis_index("comp"))
    rows, slot, bcol, brow, wrow, own = tabs
    f32 = jnp.float32
    smem = pl.BlockSpec(memory_space=pltpu.SMEM)
    vmem = pl.BlockSpec(memory_space=pltpu.VMEM)
    out = pl.pallas_call(
        functools.partial(kernel, nc, nd),
        out_shape=jax.ShapeDtypeStruct((planes, nb, nrow, lanes), f32),
        in_specs=[smem, smem, smem, vmem, vmem, vmem, vmem, vmem],
        out_specs=vmem,
        scratch_shapes=[
            pltpu.VMEM((2, planes, nb, nrow, lanes), f32),
            pltpu.VMEM((2, nb, nrow, lanes), f32),
            pltpu.VMEM((STEPS - 1, 2, nb, nrow, lanes), jnp.bfloat16),
            pltpu.VMEM((STEPS - 1, 2, nb, nrow, lanes), jnp.bfloat16),
            pltpu.VMEM((planes * nd, nrow, lanes), f32),
            pltpu.VMEM((nc, ROWS, lanes), f32),
            pltpu.VMEM((nc, ROWS, lanes), f32),
            pltpu.VMEM((nc, ROWS, lanes), f32),
            pltpu.VMEM((nc, ROWS, lanes), f32),
            pltpu.VMEM((ROWS, nrow, lanes), f32),
            pltpu.VMEM((planes * nd, nrow, lanes), f32),
            pltpu.VMEM((nd, planes, nrow, lanes), f32),
            pltpu.VMEM((nc * ROWS, nc * ROWS), jnp.bfloat16),
            pltpu.SemaphoreType.DMA((STEPS, 2, CHUNKS)),
            pltpu.SemaphoreType.DMA((STEPS, 2, CHUNKS)),
            pltpu.SemaphoreType.DMA((4, max(nc, nd))),
            pltpu.SemaphoreType.DMA((4, max(nc, nd))),
        ],
        compiler_params=pltpu.CompilerParams(collective_id=0, has_side_effects=True),
    )(rows, slot, own, bcol, brow, wrow, density[0], velocity[0])
    return out[None]


def solution(mesh):
    in_specs = (
        P("comp", "dom", None, None, None),
        P("comp", None, "dom", None, None, None),
        P(),
        P(),
    )
    out_specs = P("comp", "dom", None, None, None)
    return jax.shard_map(local, mesh=mesh, in_specs=in_specs, out_specs=out_specs, check_vma=False)
```

time: 321 us -> 94.2 us (0.29)
  the two profiles are of different devices: /device:TPU:1 before, /device:TPU:24 now
where the time goes in v1:
time: 94.2 us; the launch traced here: 93.9 us
  Pallas kernels  81 us (86%)
  local copies, waits for them, and re-layouts  6.67 us (7%)
  other arithmetic  6.19 us (7%)
    pallas_call x1, Pallas kernels, local(): pl.pallas_call(functools.partial(kernel, nc, nd), out_shape=jax.ShapeDtyp...  81 us
    reduce_sum x1, other arithmetic, tables(): block = jnp.sum(hit, axis=(1, 2)).reshape(n_comp, n_slab)  3.15 us

profile of v1, /device:TPU:24, one launch (start us, length us, event | category | flops | bytes accessed | tf_op | source)
XLA Modules:
  0.0 93.9 jit_solution(11504769634803039128)
XLA Ops:
  0.0 1.2 %dynamic_slice.15.own_ref = s32[1]{0:T(128)} dynamic-slice(s32[16]{0:T(128)} %param.6, s32[]{:T(128)S(6)} %select_n.36), dynamic_slice_sizes={1} | dynamic-slice | bytes 12 | tf_op jit(solution)/shard_map/dynamic_slice | solution.py:49
  1.2 0.7 compare_reduce_fusion
  2.0 0.7 broadcast_in_dim.91
  2.7 0.6 reshape.38.wrow_ref
  3.3 0.8 broadcast_select_fusion
  4.1 0.1 copy.8
  4.2 3.2 %select_reduce_fusion = s32[512]{0:T(512)S(1)} fusion(s32[388]{0:T(512)S(1)} %iota_add_fusion, s32[388,16]{1,0:T(8,128)S(1)} %copy.8), kind=kLoop, calls=%fused_computation | loop fusion | flops 9534976 | bytes 28432 | tf_op jit(solution)/shard_map/reduce_sum | solution.py:26
  7.4 0.1 reshape.36
  7.5 0.4 select_reduce_fusion.1
  7.8 0.6 fusion.2.slot_ref
  8.4 0.6 select_reduce_fusion.2
  9.0 0.6 fusion.1.rows_ref
  9.6 0.7 reshape.37.brow_ref
  10.3 0.8 reshape_reshape.4.bcol_ref
  11.0 81.0 %shard_map.46 = f32[2,16,16,256]{3,2,1,0:T(8,128)} custom-call(s32[16]{0:T(128)} %fusion.1.rows_ref, s32[32]{0:T(128)} %fusion.2.slot_ref, s32[1]{0:T(128)} %dynamic_slice.15.own_ref, s32[256,1]{1,0:T(8,128)} %reshape_reshape.4.bcol_ref, s32[1,256]{1,0:T(1,128)} %reshape.37.brow_ref, s32[1,256]{1,0:T(1,128)} %reshape.38.wrow_ref, ...), custom_call_target="tpu_custom_call" | custom-call | tf_op jit(solution)/shard_map/pallas_call | solution.py:329
  92.0 1.9 %copy.11 = f32[1,2,16,16,256]{4,3,2,1,0:T(8,128)} copy(f32[1,2,16,16,256]{4,3,2,1,0:T(8,128)} %bitcast.7) | data formatting | bytes 1048576
  (3 shorter events, 0.0 us)

commit v2 on v1

--- a/solution.py
+++ b/solution.py
@@ -16,38 +16,88 @@
 CHUNKS = 4
 
 
-def tables(owner_lists, coefficients, n_comp, n_slab, me):
-    blocks = owner_lists.shape[0]
-    shared = owner_lists[:, 1:2] >= 0
-    keys = jnp.where(shared, owner_lists, -1)
-    ids = jnp.arange(1, blocks + 1, dtype=jnp.int32)
-    slabs = jnp.arange(n_comp * n_slab, dtype=jnp.int32)
-    hit = jnp.where(keys[None] == slabs[:, None, None], ids[None, :, None], 0)
-    block = jnp.sum(hit, axis=(1, 2)).reshape(n_comp, n_slab)
-    multi = block > 0
-    place = jnp.arange(n_slab, dtype=jnp.int32)
-    before = place[None, :] < place[:, None]
-    rank = jnp.sum(jnp.where(before[None] & multi[:, None, :], 1, 0), axis=2)
-    slot = jnp.arange(ROWS, dtype=jnp.int32)
-    chosen = multi[:, None, :] & (rank[:, None, :] == slot[None, :, None])
-    row_block = jnp.sum(jnp.where(chosen, block[:, None, :], 0), axis=2)
-    row_place = jnp.sum(jnp.where(chosen, place[None, None, :], 0), axis=2)
-    my_rows = lax.dynamic_slice_in_dim(row_place, me, 1)[0]
-    my_slot = jnp.where(
-        lax.dynamic_slice_in_dim(multi, me, 1)[0],
-        lax.dynamic_slice_in_dim(rank, me, 1)[0],
-        USED,
-    )
-    weight = jnp.broadcast_to(coefficients[:, None], (n_comp, ROWS))
-    flat = row_block.reshape(1, -1)
-    return (
-        my_rows,
-        my_slot,
-        flat.reshape(-1, 1),
-        flat,
-        weight.reshape(1, -1),
-        lax.dynamic_slice_in_dim(coefficients, me, 1),
-    )
+def fold(x, axis, op):
+    shift = x.shape[axis] // 2
+    while shift:
+        x = op(x, pltpu.roll(x, shift, axis))
+        shift //= 2
+    return x
+
+
+def tables(lists_ref, coef_ref, padded, table, comb, mix, nc, ns):
+    i32 = jnp.int32
+    depth, blocks = lists_ref.shape
+    lane = lax.broadcasted_iota(i32, (8, 128), 1)
+    sub = lax.broadcasted_iota(i32, (8, 128), 0)
+    tiles = max(1, nc * ns // 128)
+    per = 128 // ns
+    total = nc * ns
+
+    padded[...] = jnp.full(padded.shape, -1, i32)
+    padded[:, pl.ds(0, blocks)] = lists_ref[...]
+    slab = lax.broadcasted_iota(i32, (total, 128), 0)
+    wide = lax.broadcasted_iota(i32, (total, 128), 1)
+    number = jnp.zeros((total, 128), i32)
+    for t in range(padded.shape[1] // 128):
+        rows = padded[:, pl.ds(t * 128, 128)]
+        own = jnp.broadcast_to(rows[:, None, :], (nc, ns, 128)).reshape(total, 128)
+        found = (rows[0:1] == slab) | (rows[1:2] == slab) | (own == slab)
+        found = found & (rows[1:2] >= 0)
+        number = jnp.maximum(number, jnp.where(found, wide + (t * 128 + 1), 0))
+    number = fold(number, 1, jnp.maximum)
+    number = jnp.where(wide == slab % 128, number, 0)
+
+    ident = jnp.zeros((8, 128), i32)
+    for r in range(tiles):
+        part = number[r * 128 : min(r * 128 + 128, total)]
+        part = jnp.sum(part.reshape(-1, 8, 128), axis=0)
+        ident = jnp.where(sub == r, fold(part, 0, jnp.add), ident)
+    place = lane % ns
+    one = jnp.where(ident > 0, 1, 0)
+    count = one
+    shift = 1
+    while shift < ns:
+        count = count + jnp.where(place >= shift, pltpu.roll(count, shift, 1), 0)
+        shift *= 2
+    slot = jnp.where(ident > 0, count - 1, USED)
+    table[pl.ds(0, 8), :] = slot
+    both = jnp.where(ident > 0, ident * 64 + place, 0)
+    comb[pl.ds(0, 8), :] = both
+
+    lane2 = lax.broadcasted_iota(i32, (ROWS, 128), 1)
+    slot2 = lax.broadcasted_iota(i32, (ROWS, 128), 0)
+    columns = []
+    for c in range(nc):
+        r = c // per
+        row = jnp.broadcast_to(table[pl.ds(r, 1), :], (ROWS, 128))
+        val = jnp.broadcast_to(comb[pl.ds(r, 1), :], (ROWS, 128))
+        mine = (row == slot2) & (lane2 // ns == c % per)
+        columns.append(fold(jnp.where(mine, val, 0), 1, jnp.add))
+
+    groups = 128 // ROWS
+    width = nc * ROWS
+    srow = jnp.zeros((8, 128), i32)
+    across = []
+    for t in range(0, nc, groups):
+        line = jnp.zeros((ROWS, 128), i32)
+        for c in range(t, min(t + groups, nc)):
+            diag = lane2 == slot2 + (c - t) * ROWS
+            line = line + jnp.where(diag, columns[c], 0)
+        line = fold(line[:8] + line[8:], 0, jnp.add)
+        across.append(jnp.concatenate([line, line], axis=0))
+        srow = jnp.where(sub == t // groups, line % 64, srow)
+    table[pl.ds(8, 8), :] = srow
+
+    span = min(128, width)
+    for t, wide in enumerate(across):
+        owner = lane2 // ROWS + t * groups
+        weight = jnp.zeros((ROWS, 128), i32)
+        for c in range(nc):
+            weight = jnp.where(owner == c, coef_ref[c], weight)
+        for c in range(nc):
+            same = (columns[c] // 64 == wide // 64) & (wide > 0) & (owner != c)
+            piece = jnp.where(same, weight, 0).astype(jnp.float32).astype(jnp.bfloat16)
+            mix[pl.ds(c * ROWS, ROWS), pl.ds(t * 128, span)] = piece[:, :span]
 
 
 def stencil(cur, low, high, left, right, rates, masks):
@@ -88,10 +138,10 @@
 
 def kernel(
     nc, nd,
-    rows_ref, slot_ref, own_ref, bcol_ref, brow_ref, wrow_ref, dens_ref, vel_ref,
+    coef_ref, lists_ref, dens_ref, vel_ref,
     out_ref,
-    ubuf, hfirst, hs, hr, line, tsend, tall, eback, erecv, ez, osend, orecv, mix,
-    hs_sem, hr_sem, a_sem, b_sem,
+    ubuf, hfirst, hs, hr, line, tsend, tall, eback, erecv, ez, osend, orecv, mix, padded, table, comb, tab,
+    tab_sem, hs_sem, hr_sem, a_sem, b_sem,
 ):
     mc = lax.axis_index("comp")
     md = lax.axis_index("dom")
@@ -131,14 +181,19 @@
         halo(0, 0, ch).start()
         halo(0, 1, ch).start()
 
-    same = (bcol_ref[...] == brow_ref[...]) & (brow_ref[...] > 0)
-    width = nc * ROWS
-    far = (lax.broadcasted_iota(jnp.int32, (width, width), 0) // ROWS) != (
-        lax.broadcasted_iota(jnp.int32, (width, width), 1) // ROWS
-    )
-    mix[...] = jnp.where(
-        same & far, wrow_ref[...].astype(jnp.float32), 0.0
-    ).astype(jnp.bfloat16)
+    ns = 2 * nd
+    tables(lists_ref, coef_ref, padded, table, comb, mix, nc, ns)
+    fetch = pltpu.make_async_copy(table, tab, tab_sem)
+    fetch.start()
+
+    per = 128 // ns
+
+    def slot_of(s):
+        return tab[mc // per, (mc % per) * ns + s]
+
+    def slab_of(j):
+        at = mc * ROWS + j
+        return tab[8 + at // 128, at % 128]
 
     nrow = dens_ref.shape[2]
     lane = lax.broadcasted_iota(jnp.int32, (nrow, 128), 1)
@@ -234,6 +289,7 @@
     for p in range(2):
         line[2 * md + p] = last[p, md]
     exchange_wait(*ph0, md, nd)
+    fetch.wait()
 
     for half in range(2):
         rows = []
@@ -242,7 +298,7 @@
             if j >= USED:
                 rows.append(jnp.zeros_like(line[0]))
                 continue
-            s = rows_ref[j]
+            s = slab_of(j)
             h = s & (-s)
             w = jnp.where(s == 0, 0.0, 0.5)
             n = 2 * nd
@@ -281,11 +337,11 @@
             continue
         r = (pl.ds(q % 2 * 8, min(8, nrow)), pl.ds(q // 2 * 128, 128))
         planes = {}
-        planes[0] = ez[(slot_ref[0], *r)]
+        planes[0] = ez[(slot_of(0), *r)]
         gap = n // 2
         while gap >= 1:
             for s in range(gap, n, 2 * gap):
-                planes[s] = ez[(slot_ref[s], *r)] + 0.5 * (
+                planes[s] = ez[(slot_of(s), *r)] + 0.5 * (
                     planes[(s - gap) % n] + planes[(s + gap) % n]
                 )
             gap //= 2
@@ -298,7 +354,7 @@
         orecv[md, p] = osend[2 * md + p]
     exchange_wait(*ph3, md, nd)
 
-    own = own_ref[0].astype(jnp.float32)
+    own = coef_ref[mc].astype(jnp.float32)
 
     @pl.loop(0, nb)
     def _(b):
@@ -321,15 +377,13 @@
     nc = lax.axis_size("comp")
     nd = lax.axis_size("dom")
     _, planes, nb, nrow, lanes = density.shape
-    tabs = tables(owner_lists, coefficients, nc, planes * nd, lax.axis_index("comp"))
-    rows, slot, bcol, brow, wrow, own = tabs
     f32 = jnp.float32
     smem = pl.BlockSpec(memory_space=pltpu.SMEM)
     vmem = pl.BlockSpec(memory_space=pltpu.VMEM)
     out = pl.pallas_call(
         functools.partial(kernel, nc, nd),
         out_shape=jax.ShapeDtypeStruct((planes, nb, nrow, lanes), f32),
-        in_specs=[smem, smem, smem, vmem, vmem, vmem, vmem, vmem],
+        in_specs=[smem, vmem, vmem, vmem],
         out_specs=vmem,
         scratch_shapes=[
             pltpu.VMEM((2, planes, nb, nrow, lanes), f32),
@@ -345,13 +399,18 @@
             pltpu.VMEM((planes * nd, nrow, lanes), f32),
             pltpu.VMEM((nd, planes, nrow, lanes), f32),
             pltpu.VMEM((nc * ROWS, nc * ROWS), jnp.bfloat16),
+            pltpu.VMEM((nc, pl.cdiv(owner_lists.shape[0], 128) * 128), jnp.int32),
+            pltpu.VMEM((16, 128), jnp.int32),
+            pltpu.VMEM((8, 128), jnp.int32),
+            pltpu.SMEM((16, 128), jnp.int32),
+            pltpu.SemaphoreType.DMA,
             pltpu.SemaphoreType.DMA((STEPS, 2, CHUNKS)),
             pltpu.SemaphoreType.DMA((STEPS, 2, CHUNKS)),
             pltpu.SemaphoreType.DMA((4, max(nc, nd))),
             pltpu.SemaphoreType.DMA((4, max(nc, nd))),
         ],
         compiler_params=pltpu.CompilerParams(collective_id=0, has_side_effects=True),
-    )(rows, slot, own, bcol, brow, wrow, density[0], velocity[0])
+    )(coefficients, owner_lists.T, density[0], velocity[0])
     return out[None]
 
 

time: 94.2 us -> 82.6 us (0.88)
  the two profiles are of different devices: /device:TPU:24 before, /device:TPU:1 now
where the time goes in v2:
time: 82.6 us; the launch traced here: 82.4 us
  Pallas kernels  80.5 us (97%)
  local copies, waits for them, and re-layouts  1.87 us (2%)
    pallas_call x1, Pallas kernels, local(): pl.pallas_call(functools.partial(kernel, nc, nd), out_shape=jax.ShapeDtyp...  80.5 us
    unnamed x1, local copies, waits for them, and re-layouts  1.87 us

profile of v2, /device:TPU:1, one launch (start us, length us, event | category | flops | bytes accessed | tf_op | source)
XLA Modules:
  0.0 82.4 jit_solution(17525751828519876667)
XLA Ops:
  0.0 80.5 %shard_map.46 = f32[2,16,16,256]{3,2,1,0:T(8,128)} custom-call(s32[16]{0:T(128)} %coef_ref.1, s32[16,388]{1,0:T(8,128)} %bitcast.7, f32[2,16,16,256]{3,2,1,0:T(8,128)} %bitcast.6, bf16[6,2,16,16,256]{4,3,2,1,0:T(8,128)(2,1)} %bitcast.5), custom_call_target="tpu_custom_call" | custom-call | tf_op jit(solution)/shard_map/pallas_call | solution.py:383
  80.5 1.9 %copy.6 = f32[1,2,16,16,256]{4,3,2,1,0:T(8,128)} copy(f32[1,2,16,16,256]{4,3,2,1,0:T(8,128)} %bitcast.4) | data formatting | bytes 1048576

commit v3 on v2

--- a/solution.py
+++ b/solution.py
@@ -98,6 +98,28 @@
             same = (columns[c] // 64 == wide // 64) & (wide > 0) & (owner != c)
             piece = jnp.where(same, weight, 0).astype(jnp.float32).astype(jnp.bfloat16)
             mix[pl.ds(c * ROWS, ROWS), pl.ds(t * 128, span)] = piece[:, :span]
+
+
+def peak(values):
+    m = functools.reduce(jnp.maximum, [jnp.abs(v) for v in values])
+    if m.shape[0] > 8:
+        m = jnp.maximum(m[:8], m[8:])
+    return jnp.maximum(fold(m, 0, jnp.maximum)[0:1], 1e-30)
+
+
+def code(a, b, inverse):
+    qa = jnp.floor(a * inverse + 0.5).astype(jnp.int32)
+    qb = jnp.floor(b * inverse + 0.5).astype(jnp.int32)
+    return (qa << 16) | (qb & 0xFFFF)
+
+
+def decode(word, unit):
+    a = (word >> 16).astype(jnp.float32) * unit
+    b = ((word << 16) >> 16).astype(jnp.float32) * unit
+    return a, b
+
+
+LEVELS = 32767.0
 
 
 def stencil(cur, low, high, left, right, rates, masks):
@@ -140,13 +162,15 @@
     nc, nd,
     coef_ref, lists_ref, dens_ref, vel_ref,
     out_ref,
-    ubuf, hfirst, hs, hr, line, tsend, tall, eback, erecv, ez, osend, orecv, mix, padded, table, comb, tab,
+    ubuf, hs, hr, hs_unit, hr_unit, hdec, line, tsend, tall, eback, erecv, ez, osend,
+    out_w, in_w, out2_w, in2_w, out_u, in_u, out2_u, in2_u, mix, padded, table, comb, tab,
     tab_sem, hs_sem, hr_sem, a_sem, b_sem,
 ):
     mc = lax.axis_index("comp")
     md = lax.axis_index("dom")
     nb = dens_ref.shape[1]
-    size = nb // CHUNKS
+    chunks = min(CHUNKS, nb // 2)
+    size = nb // chunks
     up_d = lax.rem(md + 1, nd)
     dn_d = lax.rem(md + nd - 1, nd)
 
@@ -161,25 +185,51 @@
         pl.semaphore_signal(barrier, inc=1, device_id={"comp": lax.rem(mc + i, nc)})
 
     def halo(step, way, ch):
-        part = pl.ds(ch * size, size)
-        if step == 0:
-            src, dst = dens_ref.at[1 - way, part], hfirst.at[way, part]
-        else:
-            src, dst = hs.at[step - 1, way, part], hr.at[step - 1, way, part]
-        return pltpu.make_async_remote_copy(
-            src_ref=src,
-            dst_ref=dst,
-            send_sem=hs_sem.at[step, way, ch],
-            recv_sem=hr_sem.at[step, way, ch],
-            device_id={"dom": up_d if way == 0 else dn_d},
-        )
+        peer = {"dom": up_d if way == 0 else dn_d}
+        return [
+            pltpu.make_async_remote_copy(
+                src_ref=src.at[step, way, ch],
+                dst_ref=dst.at[step, way, ch],
+                send_sem=hs_sem.at[kind, step, way, ch],
+                recv_sem=hr_sem.at[kind, step, way, ch],
+                device_id=peer,
+            )
+            for kind, (src, dst) in enumerate(((hs, hr), (hs_unit, hr_unit)))
+        ]
+
+    def half(h):
+        return pl.ds(h * 128, 128)
+
+    pair = size // 2
+
+    def halo_send(src, step, ch):
+        for way in range(2):
+            for h in range(2):
+                vals = [src[1 - way, ch * size + i, :, half(h)] for i in range(size)]
+                top = peak(vals)
+                inverse = LEVELS / top
+                for i in range(pair):
+                    hs[step, way, ch, i, :, half(h)] = code(vals[i], vals[i + pair], inverse)
+                hs_unit[step, way, ch, pl.ds(h, 1), :] = top * (1.0 / LEVELS)
+            for copy in halo(step, way, ch):
+                copy.start()
+
+    def halo_receive(step, ch):
+        for way in range(2):
+            for copy in halo(step, way, ch):
+                copy.wait_recv()
+            for h in range(2):
+                unit = hr_unit[step, way, ch, pl.ds(h, 1), :]
+                for i in range(pair):
+                    first, second = decode(hr[step, way, ch, i, :, half(h)], unit)
+                    hdec[way, ch * size + i, :, half(h)] = first
+                    hdec[way, ch * size + i + pair, :, half(h)] = second
 
     pl.semaphore_wait(barrier, nd + nc - 2)
 
-    @pl.loop(0, CHUNKS)
+    @pl.loop(0, chunks)
     def _(ch):
-        halo(0, 0, ch).start()
-        halo(0, 1, ch).start()
+        halo_send(dens_ref, 0, ch)
 
     ns = 2 * nd
     tables(lists_ref, coef_ref, padded, table, comb, mix, nc, ns)
@@ -211,10 +261,9 @@
         src = dens_ref if step == 0 else ubuf.at[(step - 1) % 2]
         dst = ubuf.at[step % 2]
 
-        @pl.loop(0, CHUNKS)
+        @pl.loop(0, chunks)
         def _(ch):
-            halo(step, 0, ch).wait_recv()
-            halo(step, 1, ch).wait_recv()
+            halo_receive(step, ch)
 
             @pl.loop(0, size)
             def _(i):
@@ -223,8 +272,8 @@
                 bp = lax.rem(b + 1, nb)
                 first = halves(src, 0, b)
                 second = halves(src, 1, b)
-                lo = halves(hfirst, 0, b) if step == 0 else halves(hr, step - 1, 0, b)
-                hi = halves(hfirst, 1, b) if step == 0 else halves(hr, step - 1, 1, b)
+                lo = halves(hdec, 0, b)
+                hi = halves(hdec, 1, b)
                 for p in range(2):
                     cur = first if p == 0 else second
                     rates = [
@@ -245,56 +294,81 @@
                     )
                     for h in range(2):
                         dst[p, b, :, pl.ds(h * 128, 128)] = new[h]
-                        if step < STEPS - 1:
-                            hs[step, 1 - p, b, :, pl.ds(h * 128, 128)] = new[h].astype(
-                                jnp.bfloat16
-                            )
 
             if step < STEPS - 1:
-                halo(step + 1, 0, ch).start()
-                halo(step + 1, 1, ch).start()
+                halo_send(dst, step + 1, ch)
 
     last = ubuf.at[(STEPS - 1) % 2]
 
-    def spread(src_of, dst, phase, axis, me, peer):
-        return pltpu.make_async_remote_copy(
-            src_ref=src_of(peer),
-            dst_ref=dst(me),
-            send_sem=a_sem.at[phase, peer],
-            recv_sem=b_sem.at[phase, me],
-            device_id={axis: peer},
-        )
-
-    def incoming(src_of, dst, phase, axis, peer):
-        return pltpu.make_async_remote_copy(
-            src_ref=src_of(peer),
-            dst_ref=dst(peer),
-            send_sem=a_sem.at[phase, peer],
-            recv_sem=b_sem.at[phase, peer],
-            device_id={axis: peer},
-        )
-
-    def exchange_start(src_of, dst, phase, axis, me, n):
+    def spread(refs, phase, axis, me, peer):
+        return [
+            pltpu.make_async_remote_copy(
+                src_ref=src.at[peer],
+                dst_ref=dst.at[me],
+                send_sem=a_sem.at[phase, kind, peer],
+                recv_sem=b_sem.at[phase, kind, me],
+                device_id={axis: peer},
+            )
+            for kind, (src, dst) in enumerate(refs)
+        ]
+
+    def arrive(refs, phase, axis, me, peer):
+        for kind, (src, dst) in enumerate(refs):
+            pltpu.make_async_remote_copy(
+                src_ref=src.at[peer],
+                dst_ref=dst.at[peer],
+                send_sem=a_sem.at[phase, kind, peer],
+                recv_sem=b_sem.at[phase, kind, peer],
+                device_id={axis: peer},
+            ).wait_recv()
+
+    def exchange_start(refs, phase, axis, me, n):
         @pl.loop(1, n)
         def _(i):
-            spread(src_of, dst, phase, axis, me, lax.rem(me + i, n)).start()
-
-    def exchange_wait(src_of, dst, phase, axis, me, n):
+            for copy in spread(refs, phase, axis, me, lax.rem(me + i, n)):
+                copy.start()
+
+    def exchange_wait(refs, phase, axis, me, n):
         @pl.loop(1, n)
         def _(i):
-            incoming(src_of, dst, phase, axis, lax.rem(me + n - i, n)).wait_recv()
-
-    ph0 = (lambda d: last.at[:, d], lambda d: line.at[pl.ds(2 * d, 2)], 0, "dom")
-    exchange_start(*ph0, md, nd)
+            arrive(refs, phase, axis, me, lax.rem(me + n - i, n))
+
+    def encode_planes(first, second, d, words, units):
+        for h in range(2):
+            x, y = first(h), second(h)
+            top = peak([x, y])
+            words[d, :, half(h)] = code(x, y, LEVELS / top)
+            units[d, pl.ds(h, 1), :] = top * (1.0 / LEVELS)
+
+    ph0 = (((out_w, in_w), (out_u, in_u)), 0, "dom")
+
+    @pl.loop(1, nd)
+    def _(i):
+        d = lax.rem(md + i, nd)
+        encode_planes(
+            lambda h: last[0, d, :, half(h)], lambda h: last[1, d, :, half(h)], d, out_w, out_u
+        )
+        for copy in spread(*ph0, md, d):
+            copy.start()
+
     for p in range(2):
         line[2 * md + p] = last[p, md]
-    exchange_wait(*ph0, md, nd)
+
+    @pl.loop(1, nd)
+    def _(i):
+        d = lax.rem(md + nd - i, nd)
+        arrive(*ph0, md, d)
+        for h in range(2):
+            x, y = decode(in_w[d, :, half(h)], in_u[d, pl.ds(h, 1), :])
+            line[2 * d, :, half(h)] = x
+            line[2 * d + 1, :, half(h)] = y
+
     fetch.wait()
 
-    for half in range(2):
+    for part in range(2):
         rows = []
         for k in range(8):
-            j = half * 8 + k
+            j = part * 8 + k
             if j >= USED:
                 rows.append(jnp.zeros_like(line[0]))
                 continue
@@ -306,9 +380,9 @@
             hi = (s + h) & (n - 1)
             rows.append(line[s] - w * (line[lo] + line[hi]))
         block = jnp.stack(rows, axis=0)
-        tsend[:, pl.ds(half * 8, 8), :] = jnp.swapaxes(block, 0, 1)
-
-    ph1 = (lambda c: tsend.at[c], lambda c: tall.at[c], 1, "comp")
+        tsend[:, pl.ds(part * 8, 8), :] = jnp.swapaxes(block, 0, 1)
+
+    ph1 = (((tsend, tall),), 1, "comp")
     exchange_start(*ph1, mc, nc)
     tall[mc] = tsend[mc]
     exchange_wait(*ph1, mc, nc)
@@ -323,13 +397,13 @@
         acc = prod if acc is None else acc + prod
     eback[...] = acc.reshape(nc, ROWS, 256)
 
-    ph2 = (lambda c: eback.at[c], lambda c: erecv.at[c], 2, "comp")
+    ph2 = (((eback, erecv),), 2, "comp")
     exchange_start(*ph2, mc, nc)
     erecv[mc] = eback[mc]
     exchange_wait(*ph2, mc, nc)
 
-    for half in range(2):
-        ez[pl.ds(half * 8, 8)] = jnp.swapaxes(erecv[:, pl.ds(half * 8, 8), :], 0, 1)
+    for part in range(2):
+        ez[pl.ds(part * 8, 8)] = jnp.swapaxes(erecv[:, pl.ds(part * 8, 8), :], 0, 1)
 
     n = 2 * nd
     for q in range(4):
@@ -348,29 +422,44 @@
         for s in range(n):
             osend[(s, *r)] = planes[s]
 
-    ph3 = (lambda d: osend.at[pl.ds(2 * d, 2)], lambda d: orecv.at[d], 3, "dom")
-    exchange_start(*ph3, md, nd)
+    ph3 = (((out2_w, in2_w), (out2_u, in2_u)), 3, "dom")
+
+    @pl.loop(1, nd)
+    def _(i):
+        d = lax.rem(md + i, nd)
+        encode_planes(
+            lambda h: osend[2 * d, :, half(h)],
+            lambda h: osend[2 * d + 1, :, half(h)],
+            d, out2_w, out2_u,
+        )
+        for copy in spread(*ph3, md, d):
+            copy.start()
+
+    own = coef_ref[mc].astype(jnp.float32)
+
     for p in range(2):
-        orecv[md, p] = osend[2 * md + p]
-    exchange_wait(*ph3, md, nd)
-
-    own = coef_ref[mc].astype(jnp.float32)
-
-    @pl.loop(0, nb)
-    def _(b):
-        for p in range(2):
-            out_ref[p, b] = own * last[p, b] + orecv[b, p]
-
-    @pl.loop(0, CHUNKS)
+        out_ref[p, md] = own * last[p, md] + osend[2 * md + p]
+
+    @pl.loop(1, nd)
+    def _(i):
+        d = lax.rem(md + nd - i, nd)
+        arrive(*ph3, md, d)
+        for h in range(2):
+            both = decode(in2_w[d, :, half(h)], in2_u[d, pl.ds(h, 1), :])
+            for p in range(2):
+                out_ref[p, d, :, half(h)] = own * last[p, d, :, half(h)] + both[p]
+
+    @pl.loop(0, chunks)
     def _(ch):
         for step in range(STEPS):
-            halo(step, 0, ch).wait_send()
-            halo(step, 1, ch).wait_send()
+            for copy in halo(step, 0, ch) + halo(step, 1, ch):
+                copy.wait_send()
 
     for ph, me, k in ((ph0, md, nd), (ph1, mc, nc), (ph2, mc, nc), (ph3, md, nd)):
         @pl.loop(1, k)
         def _(i):
-            spread(*ph, me, lax.rem(me + i, k)).wait_send()
+            for copy in spread(*ph, me, lax.rem(me + i, k)):
+                copy.wait_send()
 
 
 def local(density, velocity, coefficients, owner_lists):
@@ -378,6 +467,7 @@
     nd = lax.axis_size("dom")
     _, planes, nb, nrow, lanes = density.shape
     f32 = jnp.float32
+    chunks = min(CHUNKS, nb // 2)
     smem = pl.BlockSpec(memory_space=pltpu.SMEM)
     vmem = pl.BlockSpec(memory_space=pltpu.VMEM)
     out = pl.pallas_call(
@@ -387,9 +477,9 @@
         out_specs=vmem,
         scratch_shapes=[
             pltpu.VMEM((2, planes, nb, nrow, lanes), f32),
+            *[pltpu.VMEM((STEPS, 2, chunks, nb // chunks // 2, nrow, lanes), jnp.int32)] * 2,
+            *[pltpu.VMEM((STEPS, 2, chunks, 2, 128), f32)] * 2,
             pltpu.VMEM((2, nb, nrow, lanes), f32),
-            pltpu.VMEM((STEPS - 1, 2, nb, nrow, lanes), jnp.bfloat16),
-            pltpu.VMEM((STEPS - 1, 2, nb, nrow, lanes), jnp.bfloat16),
             pltpu.VMEM((planes * nd, nrow, lanes), f32),
             pltpu.VMEM((nc, ROWS, lanes), f32),
             pltpu.VMEM((nc, ROWS, lanes), f32),
@@ -397,17 +487,18 @@
             pltpu.VMEM((nc, ROWS, lanes), f32),
             pltpu.VMEM((ROWS, nrow, lanes), f32),
             pltpu.VMEM((planes * nd, nrow, lanes), f32),
-            pltpu.VMEM((nd, planes, nrow, lanes), f32),
+            *[pltpu.VMEM((nd, nrow, lanes), jnp.int32)] * 4,
+            *[pltpu.VMEM((nd, 2, 128), f32)] * 4,
             pltpu.VMEM((nc * ROWS, nc * ROWS), jnp.bfloat16),
             pltpu.VMEM((nc, pl.cdiv(owner_lists.shape[0], 128) * 128), jnp.int32),
             pltpu.VMEM((16, 128), jnp.int32),
             pltpu.VMEM((8, 128), jnp.int32),
             pltpu.SMEM((16, 128), jnp.int32),
             pltpu.SemaphoreType.DMA,
-            pltpu.SemaphoreType.DMA((STEPS, 2, CHUNKS)),
-            pltpu.SemaphoreType.DMA((STEPS, 2, CHUNKS)),
-            pltpu.SemaphoreType.DMA((4, max(nc, nd))),
-            pltpu.SemaphoreType.DMA((4, max(nc, nd))),
+            pltpu.SemaphoreType.DMA((2, STEPS, 2, chunks)),
+            pltpu.SemaphoreType.DMA((2, STEPS, 2, chunks)),
+            pltpu.SemaphoreType.DMA((4, 2, max(nc, nd))),
+            pltpu.SemaphoreType.DMA((4, 2, max(nc, nd))),
         ],
         compiler_params=pltpu.CompilerParams(collective_id=0, has_side_effects=True),
     )(coefficients, owner_lists.T, density[0], velocity[0])

time: 82.6 us -> 73.9 us (0.89)
  Pallas kernels: 80.5 us -> 71.8 us
    pallas_call x1, Pallas kernels: 80.5 us -> 71.8 us  [local(): pl.pallas_call(functools.partial(kernel, nc, nd), out_shape=jax.ShapeDtyp...]
where the time goes in v3:
time: 73.9 us; the launch traced here: 73.7 us
  Pallas kernels  71.8 us (97%)
  local copies, waits for them, and re-layouts  1.87 us (3%)
    pallas_call x1, Pallas kernels, local(): pl.pallas_call(functools.partial(kernel, nc, nd), out_shape=jax.ShapeDtyp...  71.8 us
    unnamed x1, local copies, waits for them, and re-layouts  1.87 us

profile of v3, /device:TPU:1, one launch (start us, length us, event | category | flops | bytes accessed | tf_op | source)
XLA Modules:
  0.0 73.7 jit_solution(10966839478642965961)
XLA Ops:
  0.0 71.8 %shard_map.46 = f32[2,16,16,256]{3,2,1,0:T(8,128)} custom-call(s32[16]{0:T(128)} %coef_ref.1, s32[16,388]{1,0:T(8,128)} %bitcast.7, f32[2,16,16,256]{3,2,1,0:T(8,128)} %bitcast.6, bf16[6,2,16,16,256]{4,3,2,1,0:T(8,128)(2,1)} %bitcast.5), custom_call_target="tpu_custom_call" | custom-call | tf_op jit(solution)/shard_map/pallas_call | solution.py:473
  71.8 1.9 %copy.6 = f32[1,2,16,16,256]{4,3,2,1,0:T(8,128)} copy(f32[1,2,16,16,256]{4,3,2,1,0:T(8,128)} %bitcast.4) | data formatting | bytes 1048576

commit v4 on v3

--- a/solution.py
+++ b/solution.py
@@ -12,7 +12,8 @@
 E_STRIDE, E_EXT = 4, 8
 F_STRIDE, F_EXT = 1, 4
 ROWS = 16
-USED = 12
+HALF = 6
+ZERO = 16
 CHUNKS = 4
 
 
@@ -59,7 +60,8 @@
     while shift < ns:
         count = count + jnp.where(place >= shift, pltpu.roll(count, shift, 1), 0)
         shift *= 2
-    slot = jnp.where(ident > 0, count - 1, USED)
+    slot = count - 1 + jnp.where(count > HALF, 8 - HALF, 0)
+    slot = jnp.where(ident > 0, slot, ZERO)
     table[pl.ds(0, 8), :] = slot
     both = jnp.where(ident > 0, ident * 64 + place, 0)
     comb[pl.ds(0, 8), :] = both
@@ -120,6 +122,16 @@
 
 
 LEVELS = 32767.0
+FINE = 4096.0
+
+
+def exponent(top):
+    return jnp.ceil(jnp.log2(top) * FINE).astype(jnp.int32) + 1
+
+
+def scale(e, sign):
+    power = jnp.exp2(e.astype(jnp.float32) * (sign / FINE))
+    return power * (1.0 / 32700.0) if sign > 0 else power * 32700.0
 
 
 def stencil(cur, low, high, left, right, rates, masks):
@@ -322,16 +334,33 @@
                 device_id={axis: peer},
             ).wait_recv()
 
+    nz, nx = nd // 2, nc // 4
+
+    def swing(k, n):
+        return n // 2 + k // 2 - (k % 2) * k
+
+    def dom_peer(i, sign):
+        z = lax.rem(md % nz + sign * swing(i // 2, nz) + nz, nz)
+        y = lax.rem(md // nz + 1 - i % 2, 2)
+        return y * nz + z
+
+    def comp_peer(i, sign):
+        q = i // 2
+        x = lax.rem(mc // 4 + sign * swing(q % nx, nx) + nx, nx)
+        y = lax.rem((mc // 2) % 2 + 1 - q // nx, 2)
+        core = lax.rem(mc % 2 + 1 - i % 2, 2)
+        return (x * 2 + y) * 2 + core
+
     def exchange_start(refs, phase, axis, me, n):
-        @pl.loop(1, n)
+        @pl.loop(0, n - 1)
         def _(i):
-            for copy in spread(refs, phase, axis, me, lax.rem(me + i, n)):
+            for copy in spread(refs, phase, axis, me, comp_peer(i, 1)):
                 copy.start()
 
     def exchange_wait(refs, phase, axis, me, n):
-        @pl.loop(1, n)
+        @pl.loop(0, n - 1)
         def _(i):
-            arrive(refs, phase, axis, me, lax.rem(me + n - i, n))
+            arrive(refs, phase, axis, me, comp_peer(i, -1))
 
     def encode_planes(first, second, d, words, units):
         for h in range(2):
@@ -342,9 +371,9 @@
 
     ph0 = (((out_w, in_w), (out_u, in_u)), 0, "dom")
 
-    @pl.loop(1, nd)
+    @pl.loop(0, nd - 1)
     def _(i):
-        d = lax.rem(md + i, nd)
+        d = dom_peer(i, 1)
         encode_planes(
             lambda h: last[0, d, :, half(h)], lambda h: last[1, d, :, half(h)], d, out_w, out_u
         )
@@ -354,9 +383,9 @@
     for p in range(2):
         line[2 * md + p] = last[p, md]
 
-    @pl.loop(1, nd)
+    @pl.loop(0, nd - 1)
     def _(i):
-        d = lax.rem(md + nd - i, nd)
+        d = dom_peer(i, -1)
         arrive(*ph0, md, d)
         for h in range(2):
             x, y = decode(in_w[d, :, half(h)], in_u[d, pl.ds(h, 1), :])
@@ -365,45 +394,60 @@
 
     fetch.wait()
 
-    for part in range(2):
-        rows = []
-        for k in range(8):
-            j = part * 8 + k
-            if j >= USED:
-                rows.append(jnp.zeros_like(line[0]))
-                continue
-            s = slab_of(j)
-            h = s & (-s)
-            w = jnp.where(s == 0, 0.0, 0.5)
-            n = 2 * nd
-            lo = (s - h) & (n - 1)
-            hi = (s + h) & (n - 1)
-            rows.append(line[s] - w * (line[lo] + line[hi]))
-        block = jnp.stack(rows, axis=0)
-        tsend[:, pl.ds(part * 8, 8), :] = jnp.swapaxes(block, 0, 1)
+    for h in range(2):
+        tops = []
+        for k in range(HALF):
+            for j in (k, k + 8):
+                s = slab_of(j)
+                g = s & (-s)
+                w = jnp.where(s == 0, 0.0, 0.5)
+                low, up = (s - g) & (ns - 1), (s + g) & (ns - 1)
+                t = line[s, :, half(h)] - w * (line[low, :, half(h)] + line[up, :, half(h)])
+                tops.append(t)
+        top = functools.reduce(jnp.maximum, [jnp.abs(t) for t in tops])
+        e = exponent(jnp.maximum(top, 1e-30))
+        inverse = scale(e, -1)
+        words = [code(tops[2 * k], tops[2 * k + 1], inverse) for k in range(HALF)]
+        block = jnp.stack(words + [e, jnp.zeros_like(e)], axis=0)
+        tsend[:, :, half(h)] = jnp.swapaxes(block, 0, 1)
 
     ph1 = (((tsend, tall),), 1, "comp")
     exchange_start(*ph1, mc, nc)
     tall[mc] = tsend[mc]
     exchange_wait(*ph1, mc, nc)
 
-    t = tall[...].reshape(nc * ROWS, 256)
+    blocks = []
+    for c in range(nc):
+        blocks.extend(decode(tall[c], scale(tall[c, pl.ds(HALF, 1), :], 1)))
+    t = jnp.concatenate(blocks, axis=0)
     m = mix[...]
     acc = None
-    for part in range(3):
+    for part in range(2):
         piece = t.astype(jnp.bfloat16)
         t = t - piece.astype(jnp.float32)
         prod = jnp.dot(m, piece, preferred_element_type=jnp.float32)
         acc = prod if acc is None else acc + prod
-    eback[...] = acc.reshape(nc, ROWS, 256)
+    mark = lax.broadcasted_iota(jnp.int32, (8, 256), 0) == HALF
+    for c in range(nc):
+        x = acc[c * ROWS : c * ROWS + 8]
+        y = acc[c * ROWS + 8 : c * ROWS + 16]
+        top = fold(jnp.maximum(jnp.abs(x), jnp.abs(y)), 0, jnp.maximum)
+        e = exponent(jnp.maximum(top, 1e-30))
+        eback[c] = jnp.where(mark, e, code(x, y, scale(e, -1)))
 
     ph2 = (((eback, erecv),), 2, "comp")
     exchange_start(*ph2, mc, nc)
     erecv[mc] = eback[mc]
     exchange_wait(*ph2, mc, nc)
 
-    for part in range(2):
-        ez[pl.ds(part * 8, 8)] = jnp.swapaxes(erecv[:, pl.ds(part * 8, 8), :], 0, 1)
+    for h in range(2):
+        words = jnp.swapaxes(erecv[:, :, half(h)], 0, 1)
+        unit = scale(words[HALF], 1)
+        for k in range(HALF):
+            x, y = decode(words[k], unit)
+            ez[k, :, half(h)] = x
+            ez[k + 8, :, half(h)] = y
+    ez[ZERO] = jnp.zeros(ez.shape[1:], jnp.float32)
 
     n = 2 * nd
     for q in range(4):
@@ -424,9 +468,9 @@
 
     ph3 = (((out2_w, in2_w), (out2_u, in2_u)), 3, "dom")
 
-    @pl.loop(1, nd)
+    @pl.loop(0, nd - 1)
     def _(i):
-        d = lax.rem(md + i, nd)
+        d = dom_peer(i, 1)
         encode_planes(
             lambda h: osend[2 * d, :, half(h)],
             lambda h: osend[2 * d + 1, :, half(h)],
@@ -440,9 +484,9 @@
     for p in range(2):
         out_ref[p, md] = own * last[p, md] + osend[2 * md + p]
 
-    @pl.loop(1, nd)
+    @pl.loop(0, nd - 1)
     def _(i):
-        d = lax.rem(md + nd - i, nd)
+        d = dom_peer(i, -1)
         arrive(*ph3, md, d)
         for h in range(2):
             both = decode(in2_w[d, :, half(h)], in2_u[d, pl.ds(h, 1), :])
@@ -481,11 +525,8 @@
             *[pltpu.VMEM((STEPS, 2, chunks, 2, 128), f32)] * 2,
             pltpu.VMEM((2, nb, nrow, lanes), f32),
             pltpu.VMEM((planes * nd, nrow, lanes), f32),
-            pltpu.VMEM((nc, ROWS, lanes), f32),
-            pltpu.VMEM((nc, ROWS, lanes), f32),
-            pltpu.VMEM((nc, ROWS, lanes), f32),
-            pltpu.VMEM((nc, ROWS, lanes), f32),
-            pltpu.VMEM((ROWS, nrow, lanes), f32),
+            *[pltpu.VMEM((nc, 8, lanes), jnp.int32)] * 4,
+            pltpu.VMEM((ZERO + 1, nrow, lanes), f32),
             pltpu.VMEM((planes * nd, nrow, lanes), f32),
             *[pltpu.VMEM((nd, nrow, lanes), jnp.int32)] * 4,
             *[pltpu.VMEM((nd, 2, 128), f32)] * 4,

time: 73.9 us -> 70.2 us (0.950); the launches traced: 73.7 us -> 69.3 us
  Pallas kernels: 71.8 us -> 67.4 us
    pallas_call x1, Pallas kernels: 71.8 us -> 67.4 us  [local(): pl.pallas_call(functools.partial(kernel, nc, nd), out_shape=jax.ShapeDtyp...]
where the time goes in v4:
time: 70.2 us; the launch traced here: 69.3 us
  Pallas kernels  67.4 us (96%)
  local copies, waits for them, and re-layouts  1.87 us (3%)
    pallas_call x1, Pallas kernels, local(): pl.pallas_call(functools.partial(kernel, nc, nd), out_shape=jax.ShapeDtyp...  67.4 us
    unnamed x1, local copies, waits for them, and re-layouts  1.87 us

profile of v4, /device:TPU:1, one launch (start us, length us, event | category | flops | bytes accessed | tf_op | source)
XLA Modules:
  0.0 69.3 jit_solution(14968396660175490883)
XLA Ops:
  0.0 67.4 %shard_map.46 = f32[2,16,16,256]{3,2,1,0:T(8,128)} custom-call(s32[16]{0:T(128)} %coef_ref.1, s32[16,388]{1,0:T(8,128)} %bitcast.7, f32[2,16,16,256]{3,2,1,0:T(8,128)} %bitcast.6, bf16[6,2,16,16,256]{4,3,2,1,0:T(8,128)(2,1)} %bitcast.5), custom_call_target="tpu_custom_call" | custom-call | tf_op jit(solution)/shard_map/pallas_call | solution.py:517
  67.4 1.9 %copy.6 = f32[1,2,16,16,256]{4,3,2,1,0:T(8,128)} copy(f32[1,2,16,16,256]{4,3,2,1,0:T(8,128)} %bitcast.4) | data formatting | bytes 1048576

commit v5 on v4

--- a/solution.py
+++ b/solution.py
@@ -134,14 +134,14 @@
     return power * (1.0 / 32700.0) if sign > 0 else power * 32700.0
 
 
-def stencil(cur, low, high, left, right, rates, masks):
+def stencil(cur, beside, sign, left, right, rates, masks):
     e_last, e_first, f_last, f_first, d_low, d_high = masks
     out = []
     down = [pltpu.roll(x, 32, 1) for x in cur]
     up = [pltpu.roll(x, 96, 1) for x in cur]
     for h in range(2):
         x = cur[h]
-        pairs = [(high[h], low[h]), (right[h], left[h])]
+        pairs = [(right[h], left[h])]
         n = x.shape[0]
         pairs.append((pltpu.roll(x, n - 1, 0), pltpu.roll(x, 1, 0)))
         pairs.append(
@@ -163,10 +163,11 @@
         drift = None
         for d, (fwd, bwd) in enumerate(pairs):
             s = fwd + bwd
-            m = rates[h][d] * (fwd - bwd)
+            m = rates[h][d + 1] * (fwd - bwd)
             total = s if total is None else total + s
             drift = m if drift is None else drift + m
-        out.append(0.28 * x + 0.06 * total - 0.5 * drift)
+        near = (0.06 - sign * 0.5 * rates[h][0]) * beside[h]
+        out.append(0.28 * x + near + 0.06 * total - 0.5 * drift)
     return out
 
 
@@ -174,7 +175,7 @@
     nc, nd,
     coef_ref, lists_ref, dens_ref, vel_ref,
     out_ref,
-    ubuf, hs, hr, hs_unit, hr_unit, hdec, line, tsend, tall, eback, erecv, ez, osend,
+    ubuf, hs, hr, hs_unit, hr_unit, base, line, tsend, tall, eback, erecv, ez, osend,
     out_w, in_w, out2_w, in2_w, out_u, in_u, out2_u, in2_u, mix, padded, table, comb, tab,
     tab_sem, hs_sem, hr_sem, a_sem, b_sem,
 ):
@@ -214,34 +215,39 @@
 
     pair = size // 2
 
-    def halo_send(src, step, ch):
-        for way in range(2):
-            for h in range(2):
-                vals = [src[1 - way, ch * size + i, :, half(h)] for i in range(size)]
-                top = peak(vals)
-                inverse = LEVELS / top
-                for i in range(pair):
-                    hs[step, way, ch, i, :, half(h)] = code(vals[i], vals[i + pair], inverse)
-                hs_unit[step, way, ch, pl.ds(h, 1), :] = top * (1.0 / LEVELS)
-            for copy in halo(step, way, ch):
-                copy.start()
-
-    def halo_receive(step, ch):
-        for way in range(2):
-            for copy in halo(step, way, ch):
-                copy.wait_recv()
-            for h in range(2):
-                unit = hr_unit[step, way, ch, pl.ds(h, 1), :]
-                for i in range(pair):
-                    first, second = decode(hr[step, way, ch, i, :, half(h)], unit)
-                    hdec[way, ch * size + i, :, half(h)] = first
-                    hdec[way, ch * size + i + pair, :, half(h)] = second
+    def halo_send(step, way, ch, values):
+        for h in range(2):
+            vals = values[h]
+            top = peak(vals)
+            inverse = LEVELS / top
+            for i in range(pair):
+                hs[step, way, ch, i, :, half(h)] = code(vals[i], vals[i + pair], inverse)
+            hs_unit[step, way, ch, pl.ds(h, 1), :] = top * (1.0 / LEVELS)
+        for copy in halo(step, way, ch):
+            copy.start()
+
+    def halo_receive(step, way, ch):
+        for copy in halo(step, way, ch):
+            copy.wait_recv()
+        out = []
+        for h in range(2):
+            unit = hr_unit[step, way, ch, pl.ds(h, 1), :]
+            both = [decode(hr[step, way, ch, i, :, half(h)], unit) for i in range(pair)]
+            out.append([x for x, _ in both] + [y for _, y in both])
+        return out
 
     pl.semaphore_wait(barrier, nd + nc - 2)
 
     @pl.loop(0, chunks)
     def _(ch):
-        halo_send(dens_ref, 0, ch)
+        for way in range(2):
+            halo_send(
+                0, way, ch,
+                [
+                    [dens_ref[1 - way, ch + chunks * i, :, half(h)] for i in range(size)]
+                    for h in range(2)
+                ],
+            )
 
     ns = 2 * nd
     tables(lists_ref, coef_ref, padded, table, comb, mix, nc, ns)
@@ -268,47 +274,6 @@
 
     def halves(ref, *idx):
         return [ref[(*idx, slice(None), pl.ds(h * 128, 128))].astype(jnp.float32) for h in range(2)]
-
-    for step in range(STEPS):
-        src = dens_ref if step == 0 else ubuf.at[(step - 1) % 2]
-        dst = ubuf.at[step % 2]
-
-        @pl.loop(0, chunks)
-        def _(ch):
-            halo_receive(step, ch)
-
-            @pl.loop(0, size)
-            def _(i):
-                b = ch * size + i
-                bm = lax.rem(b + nb - 1, nb)
-                bp = lax.rem(b + 1, nb)
-                first = halves(src, 0, b)
-                second = halves(src, 1, b)
-                lo = halves(hdec, 0, b)
-                hi = halves(hdec, 1, b)
-                for p in range(2):
-                    cur = first if p == 0 else second
-                    rates = [
-                        [
-                            vel_ref[d, p, b, :, pl.ds(h * 128, 128)].astype(jnp.float32)
-                            for d in range(6)
-                        ]
-                        for h in range(2)
-                    ]
-                    new = stencil(
-                        cur,
-                        lo if p == 0 else first,
-                        second if p == 0 else hi,
-                        halves(src, p, bm),
-                        halves(src, p, bp),
-                        rates,
-                        masks,
-                    )
-                    for h in range(2):
-                        dst[p, b, :, pl.ds(h * 128, 128)] = new[h]
-
-            if step < STEPS - 1:
-                halo_send(dst, step + 1, ch)
 
     last = ubuf.at[(STEPS - 1) % 2]
 
@@ -371,14 +336,64 @@
 
     ph0 = (((out_w, in_w), (out_u, in_u)), 0, "dom")
 
-    @pl.loop(0, nd - 1)
-    def _(i):
-        d = dom_peer(i, 1)
-        encode_planes(
-            lambda h: last[0, d, :, half(h)], lambda h: last[1, d, :, half(h)], d, out_w, out_u
-        )
-        for copy in spread(*ph0, md, d):
-            copy.start()
+    for step in range(STEPS):
+        src = dens_ref if step == 0 else ubuf.at[(step - 1) % 2]
+        dst = ubuf.at[step % 2]
+
+        @pl.loop(0, nb)
+        def _(b):
+            bm = lax.rem(b + nb - 1, nb)
+            bp = lax.rem(b + 1, nb)
+            planes = [halves(src, p, b) for p in range(2)]
+            for p in range(2):
+                rates = [
+                    [vel_ref[d, p, b, :, half(h)].astype(jnp.float32) for d in range(6)]
+                    for h in range(2)
+                ]
+                new = stencil(
+                    planes[p],
+                    planes[1 - p],
+                    1.0 if p == 0 else -1.0,
+                    halves(src, p, bm),
+                    halves(src, p, bp),
+                    rates,
+                    masks,
+                )
+                for h in range(2):
+                    base[p, b, :, half(h)] = new[h]
+
+        @pl.loop(0, chunks)
+        def _(ch):
+            for p in range(2):
+                edge = halo_receive(step, p, ch)
+                sign = 0.5 if p == 0 else -0.5
+                fresh = []
+                for h in range(2):
+                    row = []
+                    for i in range(size):
+                        b = ch + chunks * i
+                        rate = vel_ref[0, p, b, :, half(h)].astype(jnp.float32)
+                        new = base[p, b, :, half(h)] + (0.06 + sign * rate) * edge[h][i]
+                        dst[p, b, :, half(h)] = new
+                        row.append(new)
+                    fresh.append(row)
+                if step < STEPS - 1:
+                    halo_send(step + 1, 1 - p, ch, fresh)
+
+            if step == STEPS - 1:
+
+                @pl.loop(0, size)
+                def _(i):
+                    b = ch + chunks * lax.rem(i + md // chunks + size // 2, size)
+                    encode_planes(
+                        lambda h: dst[0, b, :, half(h)], lambda h: dst[1, b, :, half(h)],
+                        b, out_w, out_u,
+                    )
+
+                    @pl.when(b != md)
+                    def _():
+                        for copy in spread(*ph0, md, b):
+                            copy.start()
 
     for p in range(2):
         line[2 * md + p] = last[p, md]
@@ -479,6 +494,22 @@
         for copy in spread(*ph3, md, d):
             copy.start()
 
+    @pl.loop(0, chunks)
+    def _(ch):
+        for step in range(STEPS):
+            for copy in halo(step, 0, ch) + halo(step, 1, ch):
+                copy.wait_send()
+
+    def sent(ph, me, k):
+        @pl.loop(1, k)
+        def _(i):
+            for copy in spread(*ph, me, lax.rem(me + i, k)):
+                copy.wait_send()
+
+    sent(ph0, md, nd)
+    sent(ph1, mc, nc)
+    sent(ph2, mc, nc)
+
     own = coef_ref[mc].astype(jnp.float32)
 
     for p in range(2):
@@ -493,17 +524,7 @@
             for p in range(2):
                 out_ref[p, d, :, half(h)] = own * last[p, d, :, half(h)] + both[p]
 
-    @pl.loop(0, chunks)
-    def _(ch):
-        for step in range(STEPS):
-            for copy in halo(step, 0, ch) + halo(step, 1, ch):
-                copy.wait_send()
-
-    for ph, me, k in ((ph0, md, nd), (ph1, mc, nc), (ph2, mc, nc), (ph3, md, nd)):
-        @pl.loop(1, k)
-        def _(i):
-            for copy in spread(*ph, me, lax.rem(me + i, k)):
-                copy.wait_send()
+    sent(ph3, md, nd)
 
 
 def local(density, velocity, coefficients, owner_lists):
@@ -523,7 +544,7 @@
             pltpu.VMEM((2, planes, nb, nrow, lanes), f32),
             *[pltpu.VMEM((STEPS, 2, chunks, nb // chunks // 2, nrow, lanes), jnp.int32)] * 2,
             *[pltpu.VMEM((STEPS, 2, chunks, 2, 128), f32)] * 2,
-            pltpu.VMEM((2, nb, nrow, lanes), f32),
+            pltpu.VMEM((planes, nb, nrow, lanes), f32),
             pltpu.VMEM((planes * nd, nrow, lanes), f32),
             *[pltpu.VMEM((nc, 8, lanes), jnp.int32)] * 4,
             pltpu.VMEM((ZERO + 1, nrow, lanes), f32),

time: 70.2 us -> 67.6 us (0.963); the launches traced: 69.3 us -> 67.4 us
  Pallas kernels: 67.4 us -> 65.5 us
    pallas_call x1, Pallas kernels: 67.4 us -> 65.5 us  [local(): pl.pallas_call(functools.partial(kernel, nc, nd), out_shape=jax.ShapeDtyp...]
where the time goes in v5:
time: 67.6 us; the launch traced here: 67.4 us
  Pallas kernels  65.5 us (97%)
  local copies, waits for them, and re-layouts  1.87 us (3%)
    pallas_call x1, Pallas kernels, local(): pl.pallas_call(functools.partial(kernel, nc, nd), out_shape=jax.ShapeDtyp...  65.5 us
    unnamed x1, local copies, waits for them, and re-layouts  1.87 us

profile of v5, /device:TPU:1, one launch (start us, length us, event | category | flops | bytes accessed | tf_op | source)
XLA Modules:
  0.0 67.4 jit_solution(7030300634584863400)
XLA Ops:
  0.0 65.5 %shard_map.46 = f32[2,16,16,256]{3,2,1,0:T(8,128)} custom-call(s32[16]{0:T(128)} %coef_ref.1, s32[16,388]{1,0:T(8,128)} %bitcast.7, f32[2,16,16,256]{3,2,1,0:T(8,128)} %bitcast.6, bf16[6,2,16,16,256]{4,3,2,1,0:T(8,128)(2,1)} %bitcast.5), custom_call_target="tpu_custom_call" | custom-call | tf_op jit(solution)/shard_map/pallas_call | solution.py:538
  65.5 1.9 %copy.6 = f32[1,2,16,16,256]{4,3,2,1,0:T(8,128)} copy(f32[1,2,16,16,256]{4,3,2,1,0:T(8,128)} %bitcast.4) | data formatting | bytes 1048576

commit v6 on v5

--- a/solution.py
+++ b/solution.py
@@ -215,7 +215,7 @@
 
     pair = size // 2
 
-    def halo_send(step, way, ch, values):
+    def halo_code(step, way, ch, values):
         for h in range(2):
             vals = values[h]
             top = peak(vals)
@@ -223,6 +223,8 @@
             for i in range(pair):
                 hs[step, way, ch, i, :, half(h)] = code(vals[i], vals[i + pair], inverse)
             hs_unit[step, way, ch, pl.ds(h, 1), :] = top * (1.0 / LEVELS)
+
+    def halo_start(step, way, ch):
         for copy in halo(step, way, ch):
             copy.start()
 
@@ -236,12 +238,10 @@
             out.append([x for x, _ in both] + [y for _, y in both])
         return out
 
-    pl.semaphore_wait(barrier, nd + nc - 2)
-
     @pl.loop(0, chunks)
     def _(ch):
         for way in range(2):
-            halo_send(
+            halo_code(
                 0, way, ch,
                 [
                     [dens_ref[1 - way, ch + chunks * i, :, half(h)] for i in range(size)]
@@ -253,6 +253,13 @@
     tables(lists_ref, coef_ref, padded, table, comb, mix, nc, ns)
     fetch = pltpu.make_async_copy(table, tab, tab_sem)
     fetch.start()
+
+    pl.semaphore_wait(barrier, nd + nc - 2)
+
+    @pl.loop(0, chunks)
+    def _(ch):
+        for way in range(2):
+            halo_start(0, way, ch)
 
     per = 128 // ns
 
@@ -305,8 +312,8 @@
         return n // 2 + k // 2 - (k % 2) * k
 
     def dom_peer(i, sign):
-        z = lax.rem(md % nz + sign * swing(i // 2, nz) + nz, nz)
-        y = lax.rem(md // nz + 1 - i % 2, 2)
+        z = lax.rem(md % nz + sign * swing(lax.rem(i, nz), nz) + nz, nz)
+        y = lax.rem(md // nz + 1 - i // nz, 2)
         return y * nz + z
 
     def comp_peer(i, sign):
@@ -378,7 +385,8 @@
                         row.append(new)
                     fresh.append(row)
                 if step < STEPS - 1:
-                    halo_send(step + 1, 1 - p, ch, fresh)
+                    halo_code(step + 1, 1 - p, ch, fresh)
+                    halo_start(step + 1, 1 - p, ch)
 
             if step == STEPS - 1:
 

time: 67.6 us -> 65 us (0.962)
  Pallas kernels: 65.5 us -> 63 us
    pallas_call x1, Pallas kernels: 65.5 us -> 63 us  [local(): pl.pallas_call(functools.partial(kernel, nc, nd), out_shape=jax.ShapeDtyp...]
where the time goes in v6:
time: 65 us; the launch traced here: 64.9 us
  Pallas kernels  63 us (97%)
  local copies, waits for them, and re-layouts  1.87 us (3%)
    pallas_call x1, Pallas kernels, local(): pl.pallas_call(functools.partial(kernel, nc, nd), out_shape=jax.ShapeDtyp...  63 us
    unnamed x1, local copies, waits for them, and re-layouts  1.87 us

profile of v6, /device:TPU:1, one launch (start us, length us, event | category | flops | bytes accessed | tf_op | source)
XLA Modules:
  0.0 64.9 jit_solution(3253857594847371908)
XLA Ops:
  0.0 63.0 %shard_map.46 = f32[2,16,16,256]{3,2,1,0:T(8,128)} custom-call(s32[16]{0:T(128)} %coef_ref.1, s32[16,388]{1,0:T(8,128)} %bitcast.7, f32[2,16,16,256]{3,2,1,0:T(8,128)} %bitcast.6, bf16[6,2,16,16,256]{4,3,2,1,0:T(8,128)(2,1)} %bitcast.5), custom_call_target="tpu_custom_call" | custom-call | tf_op jit(solution)/shard_map/pallas_call | solution.py:546
  63.0 1.9 %copy.6 = f32[1,2,16,16,256]{4,3,2,1,0:T(8,128)} copy(f32[1,2,16,16,256]{4,3,2,1,0:T(8,128)} %bitcast.4) | data formatting | bytes 1048576

commit v7 on v6

--- a/solution.py
+++ b/solution.py
@@ -324,13 +324,13 @@
         return (x * 2 + y) * 2 + core
 
     def exchange_start(refs, phase, axis, me, n):
-        @pl.loop(0, n - 1)
+        @pl.loop(0, n - 1, unroll=True)
         def _(i):
             for copy in spread(refs, phase, axis, me, comp_peer(i, 1)):
                 copy.start()
 
     def exchange_wait(refs, phase, axis, me, n):
-        @pl.loop(0, n - 1)
+        @pl.loop(0, n - 1, unroll=True)
         def _(i):
             arrive(refs, phase, axis, me, comp_peer(i, -1))
 
@@ -406,7 +406,7 @@
     for p in range(2):
         line[2 * md + p] = last[p, md]
 
-    @pl.loop(0, nd - 1)
+    @pl.loop(0, nd - 1, unroll=True)
     def _(i):
         d = dom_peer(i, -1)
         arrive(*ph0, md, d)
@@ -491,7 +491,7 @@
 
     ph3 = (((out2_w, in2_w), (out2_u, in2_u)), 3, "dom")
 
-    @pl.loop(0, nd - 1)
+    @pl.loop(0, nd - 1, unroll=True)
     def _(i):
         d = dom_peer(i, 1)
         encode_planes(
@@ -523,16 +523,16 @@
     for p in range(2):
         out_ref[p, md] = own * last[p, md] + osend[2 * md + p]
 
-    @pl.loop(0, nd - 1)
+    @pl.loop(0, nd - 1, unroll=True)
     def _(i):
         d = dom_peer(i, -1)
+        for copy in spread(*ph3, md, dom_peer(i, 1)):
+            copy.wait_send()
         arrive(*ph3, md, d)
         for h in range(2):
             both = decode(in2_w[d, :, half(h)], in2_u[d, pl.ds(h, 1), :])
             for p in range(2):
                 out_ref[p, d, :, half(h)] = own * last[p, d, :, half(h)] + both[p]
-
-    sent(ph3, md, nd)
 
 
 def local(density, velocity, coefficients, owner_lists):

time: 65 us -> 64.4 us (level)
  no operation moved by 1% of the time
where the time goes in v7:
time: 64.4 us; the launch traced here: 64.3 us
  Pallas kernels  62.4 us (97%)
  local copies, waits for them, and re-layouts  1.87 us (3%)
    pallas_call x1, Pallas kernels, local(): pl.pallas_call(functools.partial(kernel, nc, nd), out_shape=jax.ShapeDtyp...  62.4 us
    unnamed x1, local copies, waits for them, and re-layouts  1.87 us

profile of v7, /device:TPU:1, one launch (start us, length us, event | category | flops | bytes accessed | tf_op | source)
XLA Modules:
  0.0 64.3 jit_solution(15791877709961293450)
XLA Ops:
  0.0 62.4 %shard_map.46 = f32[2,16,16,256]{3,2,1,0:T(8,128)} custom-call(s32[16]{0:T(128)} %coef_ref.1, s32[16,388]{1,0:T(8,128)} %bitcast.7, f32[2,16,16,256]{3,2,1,0:T(8,128)} %bitcast.6, bf16[6,2,16,16,256]{4,3,2,1,0:T(8,128)(2,1)} %bitcast.5), custom_call_target="tpu_custom_call" | custom-call | tf_op jit(solution)/shard_map/pallas_call | solution.py:546
  62.4 1.9 %copy.6 = f32[1,2,16,16,256]{4,3,2,1,0:T(8,128)} copy(f32[1,2,16,16,256]{4,3,2,1,0:T(8,128)} %bitcast.4) | data formatting | bytes 1048576
